TPU v7x, 128 devices: a whole 4x4x4 slice. The times are simulated.
128 devices in a mesh: grp: 8 (over x, core), seq: 16 (over y, z).
Axes of the slice: x: 4, y: 4, z: 4, core: 2. Of those that a mesh axis runs over, the one named last changes fastest.
Arguments:
- tokens: bfloat16 [32, 4, 5120], P(None, None, ('grp', 'seq')), may hold values from -90 to 90
- lengths: int32 [32], replicated, may hold values from 1 to 16384, as said below
- group_perm: int32 [32], replicated, may hold values from 0 to 31, as said below
- page_table: int32 [32, 128], replicated, may hold values from 0 to 31, as said below
- k_pool: bfloat16 [4096, 128, 1024], P(('grp', 'seq')), may hold values from -17 to 17
- v_pool: bfloat16 [4096, 128, 1024], P(('grp', 'seq')), may hold values from -7 to 7
- gain_in: float32 [5120], P(('grp', 'seq')), may hold values from 0.25 to 1.75
- qkv_weight: bfloat16 [5120, 7168], P('grp', 'seq'), may hold values from -0.15625 to 0.15625
- qkv_bias: float32 [7168], P('seq'), may hold values from -16 to 16
- o_weight: bfloat16 [5120, 5120], P('seq', 'grp'), may hold values from -0.078125 to 0.078125
- gain_mid: float32 [5120], P(('grp', 'seq')), may hold values from 0.25 to 1.75
- gate_weight: bfloat16 [5120, 13824], P('grp', 'seq'), may hold values from -0.078125 to 0.078125
- up_weight: bfloat16 [5120, 13824], P('grp', 'seq'), may hold values from -0.078125 to 0.078125
- down_weight: bfloat16 [13824, 5120], P('seq', 'grp'), may hold values from -0.0546875 to 0.0546875
Outputs:
- mixed: bfloat16 [32, 4, 5120], P(None, None, ('grp', 'seq'))
Inputs may be any that keep to these rules, and one draw needn't show every extreme that they name: `lengths`: one request holds exactly 16384 cached tokens. A permutation of the requests; request group_perm[i] belongs to group i // 4. `page_table`: page p of request r lies on the device with grp index g and seq index p // 8, where g is the group of r; the slots named for one device are all different.
All inputs are finite; a program needn't handle non-finite values.
Results may differ from a plain program's by a relative error of at most 0.015.
Values may be sent and summed in bfloat16 or wider, within the bound.
No kernel may reach another device: no remote copies, remote signals or barrier semaphores. Data moves between devices by JAX's collectives and lax.ppermute only.
A program may use at most 128 MiB of HBM per device.

v0:
```python
import jax
import jax.numpy as jnp
from jax import lax
from jax.sharding import PartitionSpec as P

D = 5120
HEADS = 40
KV_HEADS = 8
HEAD_DIM = 128
STEPS = 4
REQ_GRP = 4
SHARD_PAGES = 8
PAGE = 128
BLOCK_PAGES = 4


EPSILON = 1e-06
LOW_SCORE = -1e30
ROPE_BASE = 1000000.0


def rotary(values, position):
    half_dim = values.shape[-1] // 2
    exponent = jnp.arange(half_dim, dtype=jnp.float32) * (2.0 / values.shape[-1])
    inverse = jnp.exp(-exponent * jnp.log(jnp.float32(ROPE_BASE)))
    angle = position[..., None, None] * inverse
    cosine = jnp.cos(angle)
    sine_part = jnp.sin(angle)
    first_half = values[..., :half_dim]
    second_half = values[..., half_dim:]
    return jnp.concatenate(
        [
            first_half * cosine - second_half * sine_part,
            second_half * cosine + first_half * sine_part,
        ],
        axis=-1,
    )


def absorb(carried, query_mat, key_block, value_block, live_mask, score_scale):
    best_score, weight_sums, weighted = carried
    scores = (
        jnp.einsum("hqd,khd->hqk", query_mat, key_block, preferred_element_type=jnp.float32)
        * score_scale
    )
    scores = jnp.where(live_mask, scores, LOW_SCORE)
    fresh_top = jnp.maximum(best_score, jnp.max(scores, axis=-1))
    rescale = jnp.exp(best_score - fresh_top)
    weights = jnp.where(live_mask, jnp.exp(scores - fresh_top[..., None]), 0.0)
    weight_sums = weight_sums * rescale + jnp.sum(weights, axis=-1)
    weighted = weighted * rescale[..., None] + jnp.einsum(
        "hqk,khd->hqd",
        weights.astype(jnp.bfloat16),
        value_block,
        preferred_element_type=jnp.float32,
    )
    return (fresh_top, weight_sums, weighted)


def body(
    tokens,
    lengths,
    group_perm,
    page_table,
    k_pool,
    v_pool,
    gain_in,
    qkv_weight,
    qkv_bias,
    o_weight,
    gain_mid,
    gate_weight,
    up_weight,
    down_weight,
):
    n_seq = lax.axis_size("seq")
    grp_idx = lax.axis_index("grp")
    seq_idx = lax.axis_index("seq")
    group_q = HEADS // KV_HEADS
    query_rows = STEPS * group_q
    q_width = HEADS * HEAD_DIM
    kv_width = KV_HEADS * HEAD_DIM
    score_scale = HEAD_DIM ** (-0.5)
    sorted_rows = jnp.take(tokens, group_perm, axis=0).astype(jnp.float32)
    squares_in = lax.psum(jnp.sum(sorted_rows * sorted_rows, axis=-1), ("grp", "seq"))
    normed_in = (sorted_rows * lax.rsqrt(squares_in / D + EPSILON)[..., None] * gain_in).astype(
        jnp.bfloat16
    )
    proj_part = jnp.einsum(
        "rtc,ck->rtk",
        lax.all_gather(normed_in, "seq", axis=2, tiled=True),
        qkv_weight,
        preferred_element_type=jnp.float32,
    )
    proj_share = (
        lax.psum_scatter(
            proj_part.astype(jnp.bfloat16), "grp", scatter_dimension=0, tiled=True
        ).astype(jnp.float32)
        + qkv_bias
    )
    proj_full = lax.all_gather(proj_share, "seq", axis=2, tiled=True)
    members = lax.dynamic_slice_in_dim(group_perm, grp_idx * REQ_GRP, REQ_GRP)
    my_lengths = jnp.take(lengths, members)
    steps_range = jnp.arange(STEPS, dtype=jnp.int32)
    position = (my_lengths[:, None] + steps_range[None, :]).astype(jnp.float32)
    queries = rotary(
        proj_full[..., :q_width].reshape(REQ_GRP, STEPS, HEADS, HEAD_DIM), position
    ).astype(jnp.bfloat16)
    new_keys = rotary(
        proj_full[..., q_width : q_width + kv_width].reshape(REQ_GRP, STEPS, KV_HEADS, HEAD_DIM),
        position,
    ).astype(jnp.bfloat16)
    new_values = (
        proj_full[..., q_width + kv_width :]
        .reshape(REQ_GRP, STEPS, KV_HEADS, HEAD_DIM)
        .astype(jnp.bfloat16)
    )
    shard_rows = SHARD_PAGES * PAGE
    block_rows = BLOCK_PAGES * PAGE
    shard_base = seq_idx * shard_rows
    slot_table = lax.dynamic_slice_in_dim(
        jnp.take(page_table, members, axis=0), seq_idx * SHARD_PAGES, SHARD_PAGES, 1
    )
    is_last = seq_idx == n_seq - 1
    causal = (
        steps_range[None, :] <= (jnp.arange(query_rows, dtype=jnp.int32) // group_q)[:, None]
    ) & is_last
    causal = causal[None]
    query_all = (
        queries.reshape(REQ_GRP, STEPS, KV_HEADS, group_q, HEAD_DIM)
        .transpose(0, 2, 1, 3, 4)
        .reshape(REQ_GRP, KV_HEADS, query_rows, HEAD_DIM)
    )
    live_all = jnp.clip(my_lengths - shard_base, 0, shard_rows)
    block_offsets = jnp.arange(block_rows, dtype=jnp.int32)
    best_list = []
    sums_list = []
    acc_list = []
    for member in range(REQ_GRP):
        query_mat = query_all[member]
        length = my_lengths[member]
        member_slots = slot_table[member]
        initial = (
            jnp.full((KV_HEADS, query_rows), LOW_SCORE, jnp.float32),
            jnp.zeros((KV_HEADS, query_rows), jnp.float32),
            jnp.zeros((KV_HEADS, query_rows, HEAD_DIM), jnp.float32),
        )
        carried = absorb(
            initial, query_mat, new_keys[member], new_values[member], causal, score_scale
        )
        block_count = (live_all[member] + block_rows - 1) // block_rows

        def advance(
            block_index, running, member_slots=member_slots, length=length, query_mat=query_mat
        ):
            slot_ids = lax.dynamic_slice_in_dim(
                member_slots, block_index * BLOCK_PAGES, BLOCK_PAGES
            )
            key_block = jnp.take(k_pool, slot_ids, axis=0).reshape(block_rows, KV_HEADS, HEAD_DIM)
            value_block = jnp.take(v_pool, slot_ids, axis=0).reshape(block_rows, KV_HEADS, HEAD_DIM)
            positions = shard_base + block_index * block_rows + block_offsets
            return absorb(
                running,
                query_mat,
                key_block,
                value_block,
                (positions < length)[None, None, :],
                score_scale,
            )

        carried = lax.fori_loop(0, block_count, advance, carried)
        best_list.append(carried[0])
        sums_list.append(carried[1])
        acc_list.append(carried[2])
    best_score = jnp.stack(best_list)
    weight_sums = jnp.stack(sums_list)
    weighted = jnp.stack(acc_list)
    top_score = lax.pmax(best_score, "seq")
    factor = jnp.exp(best_score - top_score)
    weight_sums, weighted = (
        lax.psum((weight_sums * factor).astype(jnp.bfloat16), "seq").astype(jnp.float32),
        lax.psum((weighted * factor[..., None]).astype(jnp.bfloat16), "seq").astype(jnp.float32),
    )
    attended = (weighted / weight_sums[..., None]).reshape(
        REQ_GRP, KV_HEADS, STEPS, group_q, HEAD_DIM
    )
    attended = (
        attended.transpose(0, 2, 1, 3, 4).reshape(REQ_GRP, STEPS, q_width).astype(jnp.bfloat16)
    )
    out_width = o_weight.shape[0]
    attended_cols = lax.dynamic_slice_in_dim(attended, seq_idx * out_width, out_width, 2)
    out_terms = jnp.einsum(
        "rtc,cd->rtd",
        lax.all_gather(attended_cols, "grp", axis=0, tiled=True),
        o_weight,
        preferred_element_type=jnp.float32,
    )
    attn_sum = lax.psum_scatter(
        out_terms.astype(jnp.bfloat16), "seq", scatter_dimension=2, tiled=True
    ).astype(jnp.float32)
    residual = sorted_rows + attn_sum
    squares_mid = lax.psum(jnp.sum(residual * residual, axis=-1), ("grp", "seq"))
    normed_mid = (residual * lax.rsqrt(squares_mid / D + EPSILON)[..., None] * gain_mid).astype(
        jnp.bfloat16
    )
    segment = lax.all_gather(normed_mid, "seq", axis=2, tiled=True)
    gate_part = jnp.einsum("rtc,cf->rtf", segment, gate_weight, preferred_element_type=jnp.float32)
    up_part = jnp.einsum("rtc,cf->rtf", segment, up_weight, preferred_element_type=jnp.float32)
    gate_sum, up_sum = (
        lax.psum(gate_part.astype(jnp.bfloat16), "grp").astype(jnp.float32),
        lax.psum(up_part.astype(jnp.bfloat16), "grp").astype(jnp.float32),
    )
    hidden = (jax.nn.silu(gate_sum) * up_sum).astype(jnp.bfloat16)
    down_terms = jnp.einsum("rtf,fd->rtd", hidden, down_weight, preferred_element_type=jnp.float32)
    down_sum = lax.psum_scatter(
        down_terms.astype(jnp.bfloat16), "seq", scatter_dimension=2, tiled=True
    ).astype(jnp.float32)
    restore = jnp.argsort(group_perm)
    return jnp.take(residual + down_sum, restore, axis=0).astype(jnp.bfloat16)


def solution(mesh):
    return jax.shard_map(
        body,
        mesh=mesh,
        in_specs=(
            P(None, None, ("grp", "seq")),
            P(),
            P(),
            P(),
            P(("grp", "seq"), None, None),
            P(("grp", "seq"), None, None),
            P(("grp", "seq")),
            P("grp", "seq"),
            P("seq"),
            P("seq", "grp"),
            P(("grp", "seq")),
            P("grp", "seq"),
            P("grp", "seq"),
            P("seq", "grp"),
        ),
        out_specs=P(None, None, ("grp", "seq")),
        check_vma=False,
    )
```

profile of v0, /device:TPU:0, one launch (start us, length us, event | category | flops | bytes accessed | tf_op | source)
XLA Modules:
  0.0 875.5 jit_solution(11767665669221930165)
XLA Ops:
  8.0 1.4 gather_fusion.8
  9.5 68.2 %psum.42 = f32[32,4]{0,1:T(4,128)S(1)} all-reduce(f32[32,4]{0,1:T(4,128)S(1)} %fusion.75), channel_id=1, replica_groups=mesh['grp'=8,'seq'=16] {'grp','seq'}, use_global_device_ids=true, to_apply=%region_2.3 | all-reduce | flops 128 | bytes 1024 | tf_op jit(solution)/shard_map/psum | solution.py:85
  78.6 21.7 %all_gather.12 = bf16[32,4,640]{0,1,2:T(4,128)(2,1)S(1)} all-gather(bf16[32,4,40]{0,1,2:T(4,128)(2,1)S(1)} %copy.177), channel_id=1, replica_groups=mesh['grp'=8,'seq'=16] {'seq'}, dimensions={2}, use_global_device_ids=true | all-gather | bytes 174080 | tf_op jit(solution)/shard_map/all_gather | solution.py:91
  100.3 2.2 convolution_convert_fusion.4
  103.4 1.3 gather_fusion.9
  104.7 1.3 gather_fusion.10
  112.0 48.4 %all-reduce.12.cloned.1.call-done = bf16[32,4,448]{2,0,1:T(8,128)(2,1)} async-done(((bf16[32,4,448]{2,0,1:T(8,128)(2,1)}), bf16[32,4,448]{2,0,1:T(8,128)(2,1)}) %all-reduce.12.cloned.1.call-update) | async-done | bytes 114704
  161.7 80.0 %all_gather.13 = f32[4,4,7168]{1,0,2:T(4,128)S(1)} all-gather(f32[4,4,448]{1,0,2:T(4,128)S(1)} %copy.179), channel_id=1, replica_groups=mesh['grp'=8,'seq'=16] {'seq'}, dimensions={2}, use_global_device_ids=true | all-gather | bytes 487424 | tf_op jit(solution)/shard_map/all_gather | solution.py:101
  241.8 4.1 convert.21
  245.8 4.5 slice.158
  251.3 9.4 %fusion.141 = (f32[4,4,40,64]{1,0,3,2:T(4,128)}, f32[4,4,40,64]{1,0,3,2:T(4,128)}) fusion(f32[4,4,40,128]{1,0,3,2:T(4,128)} %bitcast.196), kind=kLoop, calls=%fused_computation.266 | loop fusion | bytes 655360 | tf_op jit(solution)/shard_map/slice | solution.py:30
  260.7 4.1 copy.227
  264.8 4.1 copy.226
  271.7 4.4 fusion.142
  280.1 22.0 %while.63 = (s32[]{:T(128)}, f32[8,20]{1,0:T(8,128)S(1)}, f32[8,20]{1,0:T(8,128)S(1)}, f32[8,20,128]{2,1,0:T(8,128)S(1)}, s32[]{:T(128)}, /*index=5*/s32[]{:T(12...) while((s32[]{:T(128)}, f32[8,20]{1,0:T(8,128)S(1)}, ...), condition=%wide.region_27.29_spmd.clone, body=%wide.region_24.28_spmd.clone.sunk | while | flops 43772256 | bytes 15884615 | solution.py:171
  280.9 4.0 gather_fusion.7
  284.9 4.0 gather_fusion.6
  291.9 4.0 gather_fusion.7
  295.9 4.0 gather_fusion.6
  302.2 1.3 exponential_multiply_fusion.2
  303.7 22.1 %while.61 = (s32[]{:T(128)}, f32[8,20]{1,0:T(8,128)S(1)}, f32[8,20]{1,0:T(8,128)S(1)}, f32[8,20,128]{2,1,0:T(8,128)S(1)}, s32[]{:T(128)}, /*index=5*/s32[]{:T(12...) while((s32[]{:T(128)}, f32[8,20]{1,0:T(8,128)S(1)}, ...), condition=%wide.region_15.17_spmd.clone, body=%wide.region_12.16_spmd.clone.sunk | while | flops 43772256 | bytes 15884615 | solution.py:171
  304.6 4.0 gather_fusion.3
  308.6 4.0 gather_fusion.2
  315.6 4.0 gather_fusion.3
  319.6 4.0 gather_fusion.2
  326.8 25.7 %while.62 = (s32[]{:T(128)}, f32[8,20]{1,0:T(8,128)S(1)}, f32[8,20]{1,0:T(8,128)S(1)}, f32[8,20,128]{2,1,0:T(8,128)S(1)}, s32[]{:T(128)}, /*index=5*/s32[]{:T(12...) while((s32[]{:T(128)}, f32[8,20]{1,0:T(8,128)S(1)}, ...), condition=%wide.region_21.23_spmd.clone, body=%wide.region_18.22_spmd.clone.sunk | while | flops 43772256 | bytes 16048483 | solution.py:171
  328.7 4.0 gather_fusion.5
  332.7 4.0 gather_fusion.4
  341.6 4.0 gather_fusion.5
  345.6 4.0 gather_fusion.4
  354.1 23.8 %while.60 = (s32[]{:T(128)}, f32[8,20]{1,0:T(8,128)S(1)}, f32[8,20]{1,0:T(8,128)S(1)}, f32[8,20,128]{2,1,0:T(8,128)S(1)}, s32[]{:T(128)}, /*index=5*/s32[]{:T(12...) while((s32[]{:T(128)}, f32[8,20]{1,0:T(8,128)S(1)}, ...), condition=%wide.region_9.11_spmd.clone, body=%wide.region_6.10_spmd.clone.sunk | while | flops 43772256 | bytes 16048483 | solution.py:171
  355.5 4.0 gather_fusion.1
  359.5 4.0 gather_fusion
  367.4 4.0 gather_fusion.1
  371.4 4.0 gather_fusion
  377.9 70.3 %pmax.7 = f32[4,8,20]{2,1,0:T(8,128)S(1)} all-reduce(f32[4,8,20]{2,1,0:T(8,128)S(1)} %pad_maximum_fusion), channel_id=1, replica_groups=mesh['grp'=8,'seq'=16] {'seq'}, use_global_device_ids=true, to_apply=%region_28.30 | all-reduce | flops 640 | bytes 5120 | tf_op jit(solution)/shard_map/pmax | solution.py:178
  448.3 1.7 fusion.71
  450.1 36.0 %psum.44 = bf16[4,8,20]{2,1,0:T(8,128)(2,1)S(1)} all-reduce(bf16[4,8,20]{2,1,0:T(8,128)(2,1)S(1)} %get-tuple-element.666), channel_id=1, replica_groups=mesh['grp'=8,'seq'=16] {'seq'}, use_global_device_ids=true, to_apply=%region_30.32 | all-reduce | flops 640 | bytes 2560 | tf_op jit(solution)/shard_map/psum | solution.py:181
  486.2 45.8 %all-reduce.10.cloned.1.call-done = bf16[4,8,20,128]{3,1,2,0:T(8,128)(2,1)} async-done(((bf16[4,8,20,128]{3,1,2,0:T(8,128)(2,1)}), bf16[4,8,20,128]{3,1,2,0:T(8,128)(2,1)}) %all-reduce.10.cloned.1.call-update) | async-done | bytes 163856 | tf_op jit(solution)/shard_map/psum | solution.py:182
  533.4 13.0 %all_gather.14 = bf16[32,4,320]{2,1,0:T(4,128)(2,1)S(1)} all-gather(bf16[4,4,320]{2,1,0:T(4,128)(2,1)S(1)} %constant_dynamic-slice_fusion), channel_id=1, replica_groups=mesh['grp'=8,'seq'=16] {'grp'}, dimensions={0}, use_global_device_ids=true | all-gather | bytes 92160 | tf_op jit(solution)/shard_map/all_gather | solution.py:194
  546.5 1.9 convolution_convert_fusion.2
  549.7 1.7 sort.17
  552.0 78.8 %all-reduce.14.cloned.1.call-done = bf16[32,4,640]{2,0,1:T(8,128)(2,1)} async-done(((bf16[32,4,640]{2,0,1:T(8,128)(2,1)}), bf16[32,4,640]{2,0,1:T(8,128)(2,1)}) %all-reduce.14.cloned.1.call-update) | async-done | bytes 163856
  631.8 62.7 %psum.45 = f32[32,4]{0,1:T(4,128)S(1)} all-reduce(f32[32,4]{0,1:T(4,128)S(1)} %multiply_reduce_fusion), channel_id=1, replica_groups=mesh['grp'=8,'seq'=16] {'grp','seq'}, use_global_device_ids=true, to_apply=%region_33.35 | all-reduce | flops 128 | bytes 1024 | tf_op jit(solution)/shard_map/psum | solution.py:202
  695.6 23.7 %all_gather.15 = bf16[32,4,640]{0,1,2:T(4,128)(2,1)S(1)} all-gather(bf16[32,4,40]{0,1,2:T(4,128)(2,1)S(1)} %copy.213), channel_id=1, replica_groups=mesh['grp'=8,'seq'=16] {'seq'}, dimensions={2}, use_global_device_ids=true | all-gather | bytes 174080 | tf_op jit(solution)/shard_map/all_gather | solution.py:206
  722.1 58.0 %all-reduce.18.cloned.1.call-done = (bf16[32,4,864]{2,0,1:T(8,128)(2,1)}, bf16[32,4,864]{2,0,1:T(8,128)(2,1)}) async-done(((bf16[32,4,864]{2,0,1:T(8,128)(2,1)}, bf16[32,4,864]{2,0,1:T(8,128)(2,1)}), (bf16[32,4,864]{2,0,1:T(8,128)(2,1)}, bf16[32,4,864]{2,0,1:T(8,128)(2,1)})) %all-reduce.18.cloned.1.call-update) | async-done | bytes 442384 | tf_op jit(solution)/shard_map/psum | solution.py:211
  780.1 2.5 convolution_convert_fusion.3
  782.7 84.0 %all-reduce.16.cloned.1.call-done = bf16[32,4,640]{2,0,1:T(8,128)(2,1)} async-done(((bf16[32,4,640]{2,0,1:T(8,128)(2,1)}), bf16[32,4,640]{2,0,1:T(8,128)(2,1)}) %all-reduce.16.cloned.1.call-update) | async-done | bytes 163856
  (218 shorter events, 56.5 us)
Async XLA Ops:
  6.5 713.1 %copy-start = (bf16[640,864]{0,1:T(8,128)(2,1)S(1)}, bf16[640,864]{0,1:T(8,128)(2,1)}, u32[]{:S(2)}) copy-start(bf16[640,864]{0,1:T(8,128)(2,1)} %param.36) | copy-start | bytes 3317764
  6.5 154.0 %all-reduce.12.cloned.1.call-start = ((), (), s32[]{:S(2)}) async-start(), calls=%async_computation.1 | async-start | bytes 262144
  7.3 70.4 %copy-start.8 = (pred[32]{0:T(512)(128)(4,1)}, pred[32]{0:T(512)(128)(4,1)S(1)}, u32[]{:S(2)}) copy-start(pred[32]{0:T(512)(128)(4,1)S(1)} %compare_and_fusion.5) | copy-start | bytes 100
  102.5 429.5 %all-reduce.10.cloned.1.call-start = ((), (), s32[]{:S(2)}) async-start(), calls=%async_computation | async-start | bytes 327680 | tf_op jit(solution)/shard_map/psum | solution.py:182
  106.8 219.1 %copy-start.5 = (pred[20,4]{0,1:T(4,128)(4,1)}, pred[20,4]{0,1:T(4,128)(4,1)S(1)}, u32[]{:S(2)}) copy-start(pred[20,4]{0,1:T(4,128)(4,1)S(1)} %fusion.119) | copy-start | bytes 244
  270.4 9.5 %copy-start.2 = (f32[8,20,4]{1,2,0:T(4,128)}, f32[8,20,4]{1,2,0:T(4,128)S(1)}, u32[]{:S(2)}) copy-start(f32[8,20,4]{1,2,0:T(4,128)S(1)} %get-tuple-element.733) | copy-start | bytes 7684
  270.8 7.8 copy-start.6
  271.1 7.5 copy-start.7
  336.7 1.2 copy-start.4
  349.6 1.2 copy-start.4
  354.0 195.6 %copy-start.11 = (s32[32]{0:T(128)S(1)}, s32[32]{0:T(128)}, u32[]{:S(2)}) copy-start(s32[32]{0:T(128)} %param.26) | copy-start | bytes 388
  354.0 276.8 %copy-start.9 = (pred[32]{0:T(512)(128)(4,1)S(1)}, pred[32]{0:T(512)(128)(4,1)}, u32[]{:S(2)}) copy-start(pred[32]{0:T(512)(128)(4,1)} %copy-done.8) | copy-start | bytes 100
  354.1 340.5 %copy-start.10 = (f32[40]{0:T(128)S(1)}, f32[40]{0:T(128)}, u32[]{:S(2)}) copy-start(f32[40]{0:T(128)} %param.34) | copy-start | bytes 484
  363.5 0.8 copy-start.3
  375.4 0.8 copy-start.3
  377.9 343.0 %copy-start.1 = (bf16[640,864]{0,1:T(8,128)(2,1)S(1)}, bf16[640,864]{0,1:T(8,128)(2,1)}, u32[]{:S(2)}) copy-start(bf16[640,864]{0,1:T(8,128)(2,1)} %param.35) | copy-start | bytes 3317764
  450.1 180.8 %all-reduce.14.cloned.1.call-start = ((), (), s32[]{:S(2)}) async-start(), calls=%async_computation.2 | async-start | bytes 327680
  548.4 231.7 %all-reduce.18.cloned.1.call-start = ((), (), s32[]{:S(2)}) async-start(), calls=%async_computation.4 | async-start | bytes 917504 | tf_op jit(solution)/shard_map/psum | solution.py:211
  722.0 144.6 %all-reduce.16.cloned.1.call-start = ((), (), s32[]{:S(2)}) async-start(), calls=%async_computation.3 | async-start | bytes 327680
Sparse Core Ops, SparseCore 0:
  102.6 57.7 all-reduce.11
  450.2 81.8 all-reduce.9
  548.5 82.2 all-reduce.13
  722.1 57.8 all-reduce.17
  783.1 83.4 all-reduce.15
where the time goes:
time: 878 us; the launch traced here: 875 us
  blocking collectives  376 us (43%)
  waiting for transfers between devices  315 us (36%)
  local copies, waits for them, and re-layouts  111 us (13%)
  other arithmetic  34.2 us (4%)
  matrix products  21.1 us (2%)
  between operations  17.5 us (2%)
    unnamed x8, waiting for transfers between devices  211 us
    all_gather x1, blocking collectives, body(): proj_full = lax.all_gather(proj_share, 'seq', axis=2, tiled=True)  80 us
    pmax x1, blocking collectives, body(): top_score = lax.pmax(best_score, 'seq')  70.3 us
    psum x1, blocking collectives, body(): lax.psum(jnp.sum(sorted_rows * sorted_rows, axis=-1), ('grp', 'seq'))  68.2 us
    psum x1, blocking collectives, body(): lax.psum(jnp.sum(residual * residual, axis=-1), ('grp', 'seq'))  62.7 us
    psum x1, waiting for transfers between devices, body(): lax.psum(up_part.astype(jnp.bfloat16), 'grp').astype(jnp.float32)  58 us
    psum x1, waiting for transfers between devices, body(): lax.psum((weighted * factor[..., None]).astype(jnp.bfloat16), 'seq')  45.8 us
    psum x1, blocking collectives, body(): lax.psum((weight_sums * factor).astype(jnp.bfloat16), 'seq')  36 us
  transfers between devices with their start and end apart: 5, of which 5 were waited for; matrix products, arithmetic and copies ran while one was open for 1% of the time, Pallas kernels for 0%

commit v1 on v0

v1 whole, which is shorter than its diff:
```python
import functools

import jax
import jax.numpy as jnp
import numpy as np
from jax import lax
from jax.experimental import pallas as pl
from jax.experimental.pallas import tpu as pltpu
from jax.sharding import PartitionSpec as P

D = 5120
HEADS = 40
KV_HEADS = 8
HEAD_DIM = 128
STEPS = 4
REQ_GRP = 4
SHARD_PAGES = 8
PAGE = 128
REQUESTS = 32
ROWS = REQUESTS * STEPS
GROUP_ROWS = REQ_GRP * STEPS
N_GRP = 8
N_SEQ = 16
FEAT = D // (N_GRP * N_SEQ)
FEAT_PAD = 48
GFEAT = D // N_GRP
QCOLS = 448
QPAD = 512
OCOLS = 320
FCOLS = 864
FPAD = 896
QROWS = 24
SHARD_KEYS = SHARD_PAGES * PAGE
EPSILON = 1e-06
LOW_SCORE = -1e30
ROPE_BASE = 1000000.0
BF = jnp.bfloat16
F32 = jnp.float32


def call(kernel, outs, *args, smem=(), anys=(), scratch=()):
    specs = []
    for i in range(len(args)):
        if i in smem:
            specs.append(pl.BlockSpec(memory_space=pltpu.SMEM))
        elif i in anys:
            specs.append(pl.BlockSpec(memory_space=pl.ANY))
        else:
            specs.append(pl.BlockSpec(memory_space=pltpu.VMEM))
    many = isinstance(outs, (list, tuple))
    vm = pl.BlockSpec(memory_space=pltpu.VMEM)
    return pl.pallas_call(
        kernel,
        out_shape=outs,
        in_specs=specs,
        out_specs=[vm] * len(outs) if many else vm,
        scratch_shapes=list(scratch),
        name=getattr(kernel, "__name__", "kernel"),
        compiler_params=pltpu.CompilerParams(vmem_limit_bytes=48 << 20),
    )(*args)


def sds(shape, dtype=BF):
    return jax.ShapeDtypeStruct(shape, dtype)


def split(value):
    hi = value.astype(BF).astype(F32)
    return hi, value - hi


def iota(shape, axis):
    return lax.broadcasted_iota(jnp.int32, shape, axis)


def spread_features(value, squares, out_ref):
    hi, lo = split(squares)
    tail = jnp.where(iota((8, ROWS), 0) == 0, hi, jnp.where(iota((8, ROWS), 0) == 1, lo, 0.0))
    block = jnp.concatenate([value, tail], axis=0).astype(BF)
    for s in range(N_SEQ):
        out_ref[s] = block


def start_kernel(perm_ref, tok_ref, gain_ref, send_ref, xt_ref, hot_ref):
    lane = iota((8, ROWS), 1)
    source = lane & (STEPS - 1)
    for n in range(REQUESTS):
        source = source + jnp.where((lane >> 2) == n, perm_ref[n] * STEPS, 0)
    hot = jnp.where(iota((ROWS, ROWS), 0) == source[0:1, :], 1.0, 0.0).astype(BF)
    hot_ref[...] = hot
    xt = lax.dot_general(tok_ref[...], hot, (((0,), (0,)), ((), ())), preferred_element_type=F32)
    xt_ref[...] = xt
    squares = jnp.sum(xt * xt, axis=0, keepdims=True)
    spread_features(xt * gain_ref[...], squares, send_ref)


def collect_features(in_ref, scratch):
    squares = jnp.zeros((1, ROWS), F32)
    for s in range(N_SEQ):
        block = in_ref[s].astype(F32)
        scratch[s * FEAT : (s + 1) * FEAT, :] = block[:FEAT]
        squares = squares + block[FEAT : FEAT + 1] + block[FEAT + 1 : FEAT + 2]
    value = scratch[...].T.astype(BF)
    squares = jnp.broadcast_to(squares, (ROWS, ROWS)).T
    return value, squares


def qkv_kernel(in_ref, w_ref, out_ref, scratch):
    value, squares = collect_features(in_ref, scratch)
    part = jnp.dot(value, w_ref[...], preferred_element_type=F32)
    hi, lo = split(squares)
    for g in range(N_GRP):
        rows = slice(g * GROUP_ROWS, (g + 1) * GROUP_ROWS)
        out_ref[g, :, :QCOLS] = part[rows].astype(BF)
        out_ref[g, :, QCOLS:] = jnp.where(
            iota((GROUP_ROWS, QPAD - QCOLS), 1) < 32, hi[rows, : QPAD - QCOLS], lo[rows, : QPAD - QCOLS]
        ).astype(BF)


def scale_of(total, at):
    squares = total[:, at : at + 1] + total[:, at + 16 : at + 17]
    return lax.rsqrt(squares / D + EPSILON)


def qkv_sum_kernel(in_ref, bias_ref, out_ref):
    total = in_ref[0].astype(F32)
    for g in range(1, N_GRP):
        total = total + in_ref[g].astype(F32)
    squares = total[:, QCOLS : QCOLS + 1] + total[:, QCOLS + 32 : QCOLS + 33]
    scale = lax.rsqrt(squares / D + EPSILON)
    value = total * scale + bias_ref[...]
    value = jnp.where(iota(value.shape, 1) < QCOLS, value, 0.0)
    odd = lax.rem(lax.axis_index("seq"), 2) == 1
    value = jnp.where(odd, pltpu.roll(value, QPAD - QCOLS, 1), value).astype(BF)
    for s in range(N_SEQ):
        out_ref[s] = value


def attend_kernel(
    perm_ref, len_ref, page_ref, in_ref, cos_ref, sin_ref, k_hbm, v_hbm, out_ref,
    kbuf, vbuf, qbuf, knew, vnew, rot, sems,
):
    grp_idx = lax.axis_index("grp")
    seq_idx = lax.axis_index("seq")

    def copies(r, p):
        slot = page_ref[perm_ref[grp_idx * REQ_GRP + r], seq_idx * SHARD_PAGES + p]
        rows = pl.ds(p * PAGE, PAGE)
        return (
            pltpu.make_async_copy(k_hbm.at[slot], kbuf.at[r, rows], sems.at[r, p, 0]),
            pltpu.make_async_copy(v_hbm.at[slot], vbuf.at[r, rows], sems.at[r, p, 1]),
        )

    for r in range(REQ_GRP):
        for p in range(SHARD_PAGES):
            for copy in copies(r, p):
                copy.start()

    for r in range(REQ_GRP):
        member = perm_ref[grp_idx * REQ_GRP + r]
        rot[0, r * STEPS : (r + 1) * STEPS, :] = cos_ref[member]
        rot[1, r * STEPS : (r + 1) * STEPS, :] = sin_ref[member]
    cosine = rot[0]
    sine = rot[1]
    knew[...] = jnp.zeros_like(knew)
    vnew[...] = jnp.zeros_like(vnew)
    qbuf[...] = jnp.zeros_like(qbuf)
    for pair in range(N_SEQ // 2):
        even = in_ref[2 * pair].astype(F32)
        odd = in_ref[2 * pair + 1].astype(F32)
        for k in range(7):
            lanes = slice(k * 128, (k + 1) * 128)
            olanes = slice((k - 3) * 128, (k - 2) * 128)
            if k < 3:
                value = even[:, lanes]
            elif k == 3:
                value = even[:, lanes] + odd[:, olanes]
            else:
                value = odd[:, olanes]
            head = pair * 7 + k
            if head < HEADS + KV_HEADS:
                value = value * cosine + pltpu.roll(value, HEAD_DIM // 2, 1) * sine
            if head < HEADS:
                h, j = divmod(head, HEADS // KV_HEADS)
                for r in range(REQ_GRP):
                    qbuf[r, h * QROWS + j * STEPS : h * QROWS + (j + 1) * STEPS, :] = value[
                        r * STEPS : (r + 1) * STEPS
                    ]
            elif head < HEADS + KV_HEADS:
                h = head - HEADS
                knew[:GROUP_ROWS, h * HEAD_DIM : (h + 1) * HEAD_DIM] = value.astype(BF)
            else:
                h = head - HEADS - KV_HEADS
                vnew[:GROUP_ROWS, h * HEAD_DIM : (h + 1) * HEAD_DIM] = value.astype(BF)

    score_scale = HEAD_DIM ** (-0.5)
    step = iota((QROWS, PAGE), 0) & (STEPS - 1)
    column = iota((QROWS, PAGE), 1)
    place = iota((QROWS, SHARD_KEYS), 1)
    lane = iota((QROWS, HEAD_DIM), 1)
    is_last = seq_idx == N_SEQ - 1
    nt = (((1,), (1,)), ((), ()))

    def one(r, carry):
        for p in range(SHARD_PAGES):
            for copy in copies(r, p):
                copy.wait()
        live = len_ref[perm_ref[grp_idx * REQ_GRP + r]] - seq_idx * SHARD_KEYS
        live_mask = place < live
        own_mask = ((column >> 2) == r) & ((column & (STEPS - 1)) <= step) & is_last & (column < GROUP_ROWS)
        for h in range(KV_HEADS):
            lanes = slice(h * HEAD_DIM, (h + 1) * HEAD_DIM)
            query = qbuf[r, h * QROWS : (h + 1) * QROWS, :].astype(BF)
            scores = lax.dot_general(query, kbuf[r, :, lanes], nt, preferred_element_type=F32)
            scores = jnp.where(live_mask, scores * score_scale, LOW_SCORE)
            own = lax.dot_general(query, knew[:, lanes], nt, preferred_element_type=F32)
            own = jnp.where(own_mask, own * score_scale, LOW_SCORE)
            best = jnp.maximum(
                jnp.max(scores, axis=1, keepdims=True), jnp.max(own, axis=1, keepdims=True)
            )
            weight = jnp.where(live_mask, jnp.exp(scores - best), 0.0)
            own_weight = jnp.where(own_mask, jnp.exp(own - best), 0.0)
            total = jnp.sum(weight, axis=1, keepdims=True) + jnp.sum(own_weight, axis=1, keepdims=True)
            mixed = jnp.dot(
                weight.astype(BF), vbuf[r, :, lanes], preferred_element_type=F32
            ) + jnp.dot(own_weight.astype(BF), vnew[:, lanes], preferred_element_type=F32)
            some = total > 0.0
            safe = jnp.where(some, total, 1.0)
            mixed = mixed / safe
            level = jnp.where(some, best + jnp.log(safe), LOW_SCORE)
            hi, rest = split(level)
            mid, low = split(rest)
            level = jnp.where(lane < 32, hi, jnp.where(lane < 64, mid, low))
            both = jnp.concatenate([mixed[:16], level[:16]], axis=0)
            out_ref[2 * h, r] = both.astype(BF)
            both = jnp.concatenate([mixed[8:], level[8:]], axis=0)
            out_ref[2 * h + 1, r] = both.astype(BF)
        return carry

    lax.fori_loop(0, REQ_GRP, one, 0)


def merge_kernel(in_ref, out_ref, scratch):
    for r in range(REQ_GRP):
        levels = []
        for s in range(N_SEQ):
            cols = in_ref[s, r, 16:, :].astype(F32)
            levels.append(cols[:, 0:1] + cols[:, 32:33] + cols[:, 64:65])
        best = functools.reduce(jnp.maximum, levels)
        total = jnp.zeros_like(best)
        value = jnp.zeros((16, HEAD_DIM), F32)
        for s in range(N_SEQ):
            factor = jnp.exp(levels[s] - best)
            total = total + factor
            value = value + in_ref[s, r, :16, :].astype(F32) * factor
        value = value / total
        for j in range(3):
            scratch[r * STEPS : (r + 1) * STEPS, j * HEAD_DIM : (j + 1) * HEAD_DIM] = value[
                j * STEPS : (j + 1) * STEPS
            ]
    value = scratch[...]
    odd = lax.rem(lax.axis_index("seq"), 2) == 1
    value = jnp.where(odd, pltpu.roll(value, 3 * HEAD_DIM - HEAD_DIM // 2, 1), value).astype(BF)
    for g in range(N_GRP):
        out_ref[g] = value


def send_back(part, out_ref):
    turned = part.T
    for s in range(N_SEQ):
        out_ref[s] = turned[s * FEAT : (s + 1) * FEAT].astype(BF)


def project_kernel(in_ref, w_ref, out_ref):
    value = in_ref[...].reshape(ROWS, in_ref.shape[2])[:, : w_ref.shape[0]]
    send_back(jnp.dot(value, w_ref[...], preferred_element_type=F32), out_ref)


def middle_kernel(in_ref, xt_ref, gain_ref, send_ref, res_ref):
    total = xt_ref[...]
    part = in_ref[0].astype(F32)
    for s in range(1, N_SEQ):
        part = part + in_ref[s].astype(F32)
    total = total + part
    res_ref[...] = total
    squares = jnp.sum(total * total, axis=0, keepdims=True)
    spread_features(total * gain_ref[...], squares, send_ref)


def gate_kernel(in_ref, gate_ref, up_ref, out_ref, scratch):
    value, squares = collect_features(in_ref, scratch)
    gate = jnp.dot(value, gate_ref[...], preferred_element_type=F32)
    up = jnp.dot(value, up_ref[...], preferred_element_type=F32)
    hi, lo = split(squares)
    for g in range(N_GRP):
        rows = slice(g * GROUP_ROWS, (g + 1) * GROUP_ROWS)
        out_ref[g, :, :FCOLS] = gate[rows].astype(BF)
        out_ref[g, :, FCOLS:FPAD] = jnp.where(
            iota((GROUP_ROWS, FPAD - FCOLS), 1) < 16, hi[rows, : FPAD - FCOLS], lo[rows, : FPAD - FCOLS]
        ).astype(BF)
        out_ref[g, :, FPAD : FPAD + FCOLS] = up[rows].astype(BF)
        out_ref[g, :, FPAD + FCOLS :] = jnp.zeros((GROUP_ROWS, FPAD - FCOLS), BF)


def hidden_kernel(in_ref, out_ref):
    total = in_ref[0].astype(F32)
    for g in range(1, N_GRP):
        total = total + in_ref[g].astype(F32)
    scale = scale_of(total, FCOLS)
    gate = total[:, :FPAD] * scale
    up = total[:, FPAD:] * scale
    value = (gate / (1.0 + jnp.exp(-gate)) * up).astype(BF)
    for g in range(N_GRP):
        out_ref[g] = value


def finish_kernel(in_ref, res_ref, hot_ref, out_ref):
    part = in_ref[0].astype(F32)
    for s in range(1, N_SEQ):
        part = part + in_ref[s].astype(F32)
    total = (res_ref[...] + part).astype(BF)
    out_ref[...] = lax.dot_general(
        hot_ref[...], total, (((1,), (1,)), ((), ())), preferred_element_type=F32
    ).astype(BF)


def exchange(value, axis):
    return lax.all_to_all(value, axis, 0, 0, tiled=False)


def body(
    tokens, lengths, group_perm, page_table, k_pool, v_pool, gain_in, qkv_weight, qkv_bias,
    o_weight, gain_mid, gate_weight, up_weight, down_weight,
):
    half = HEAD_DIM // 2
    inverse = np.exp(-np.arange(half) * (2.0 / HEAD_DIM) * np.log(ROPE_BASE)).astype(np.float32)
    inverse = jnp.asarray(np.concatenate([inverse, inverse]))
    position = (lengths[:, None] + jnp.arange(STEPS, dtype=jnp.int32)[None, :]).astype(F32)
    angle = position[..., None] * inverse
    cosine = jnp.cos(angle)
    sine = jnp.where(jnp.arange(HEAD_DIM) < half, -1.0, 1.0) * jnp.sin(angle)

    send, xt, hot = call(
        start_kernel,
        [sds((N_SEQ, FEAT_PAD, ROWS)), sds((FEAT, ROWS), F32), sds((ROWS, ROWS))],
        group_perm, tokens.reshape(ROWS, FEAT), gain_in[:, None],
        smem=(0,),
    )
    got = exchange(send, "seq")
    send = call(
        qkv_kernel, sds((N_GRP, GROUP_ROWS, QPAD)), got, qkv_weight,
        scratch=[pltpu.VMEM((GFEAT, ROWS), F32)],
    )
    got = exchange(send, "grp")
    bias = jnp.pad(qkv_bias, (0, QPAD - QCOLS))[None, :]
    send = call(qkv_sum_kernel, sds((N_SEQ, GROUP_ROWS, QPAD)), got, bias)
    got = exchange(send, "seq")
    send = call(
        attend_kernel, sds((N_SEQ, REQ_GRP, 32, HEAD_DIM)),
        group_perm, lengths, page_table, got, cosine, sine, k_pool, v_pool,
        smem=(0, 1, 2), anys=(6, 7),
        scratch=[
            pltpu.VMEM((REQ_GRP, SHARD_KEYS, KV_HEADS * HEAD_DIM), BF),
            pltpu.VMEM((REQ_GRP, SHARD_KEYS, KV_HEADS * HEAD_DIM), BF),
            pltpu.VMEM((REQ_GRP, KV_HEADS * QROWS, HEAD_DIM), F32),
            pltpu.VMEM((PAGE, KV_HEADS * HEAD_DIM), BF),
            pltpu.VMEM((PAGE, KV_HEADS * HEAD_DIM), BF),
            pltpu.VMEM((2, GROUP_ROWS, HEAD_DIM), F32),
            pltpu.SemaphoreType.DMA((REQ_GRP, SHARD_PAGES, 2)),
        ],
    )
    got = exchange(send, "seq")
    send = call(
        merge_kernel, sds((N_GRP, GROUP_ROWS, 3 * HEAD_DIM)), got,
        scratch=[pltpu.VMEM((GROUP_ROWS, 3 * HEAD_DIM), F32)],
    )
    got = exchange(send, "grp")
    send = call(project_kernel, sds((N_SEQ, FEAT, ROWS)), got, o_weight)
    got = exchange(send, "seq")
    send, res = call(
        middle_kernel, [sds((N_SEQ, FEAT_PAD, ROWS)), sds((FEAT, ROWS), F32)],
        got, xt, gain_mid[:, None],
    )
    got = exchange(send, "seq")
    send = call(
        gate_kernel, sds((N_GRP, GROUP_ROWS, 2 * FPAD)), got, gate_weight, up_weight,
        scratch=[pltpu.VMEM((GFEAT, ROWS), F32)],
    )
    got = exchange(send, "grp")
    send = call(hidden_kernel, sds((N_GRP, GROUP_ROWS, FPAD)), got)
    got = exchange(send, "grp")
    send = call(project_kernel, sds((N_SEQ, FEAT, ROWS)), got, down_weight)
    got = exchange(send, "seq")
    out = call(finish_kernel, sds((ROWS, FEAT)), got, res, hot)
    return out.reshape(REQUESTS, STEPS, FEAT)


def solution(mesh):
    return jax.shard_map(
        body,
        mesh=mesh,
        in_specs=(
            P(None, None, ("grp", "seq")),
            P(),
            P(),
            P(),
            P(("grp", "seq"), None, None),
            P(("grp", "seq"), None, None),
            P(("grp", "seq")),
            P("grp", "seq"),
            P("seq"),
            P("seq", "grp"),
            P(("grp", "seq")),
            P("grp", "seq"),
            P("grp", "seq"),
            P("seq", "grp"),
        ),
        out_specs=P(None, None, ("grp", "seq")),
        check_vma=False,
    )
```

time: 878 us -> 144 us (0.16)
  blocking collectives: 376 us -> 55.2 us
  waiting for transfers between devices: 315 us -> 33.8 us
  local copies, waits for them, and re-layouts: 111 us -> 6.46 us
  other arithmetic: 34.2 us -> 0.61 us
  Pallas kernels: 0 us -> 23.3 us
  starting transfers between devices: 0.17 us -> 23.2 us
  matrix products: 21.1 us -> 0 us
  between operations: 17.5 us -> 0.2 us
    unnamed x8 -> x0, waiting for transfers between devices: 211 us -> none
    psum x3 -> x0, blocking collectives: 167 us -> none  [the longest x1 68.2 us: body(): lax.psum(jnp.sum(sorted_rows * sorted_rows, axis=-1), ('grp', 'seq'))]
    all_gather x4 -> x0, blocking collectives: 138 us -> none  [the longest x1 80 us: body(): proj_full = lax.all_gather(proj_share, 'seq', axis=2, tiled=True)]
    psum x2 -> x0, waiting for transfers between devices: 104 us -> none  [the longest x1 58 us: body(): lax.psum(up_part.astype(jnp.bfloat16), 'grp').astype(jnp.float32)]
    pmax x1 -> x0, blocking collectives: 70.3 us -> none  [body(): top_score = lax.pmax(best_score, 'seq')]
    gather x20 -> x0, local copies, waits for them, and re-layouts: 68.5 us -> none  [the longest x8 32 us: advance(): jnp.take(v_pool, slot_ids, axis=0).reshape(block_rows, KV_HEADS, HEAD_DIM)]
    all_to_all x0 -> x5, blocking collectives: none -> 55.2 us  [exchange(): return lax.all_to_all(value, axis, 0, 0, tiled=False)]
    all_to_all x0 -> x5, waiting for transfers between devices: none -> 33.8 us  [exchange(): return lax.all_to_all(value, axis, 0, 0, tiled=False)]
  transfers between devices with their start and end apart: 5 -> 5, of which waited for: 5 -> 5; matrix products, arithmetic and copies ran while one was open for 1% -> 3% of each run, Pallas kernels for 0% -> 0%
where the time goes in v1:
time: 144 us; the launch traced here: 143 us
  blocking collectives  55.2 us (38%)
  waiting for transfers between devices  33.8 us (23%)
  Pallas kernels  23.3 us (16%)
  starting transfers between devices  23.2 us (16%)
  local copies, waits for them, and re-layouts  6.46 us (4%)
    all_to_all x5, blocking collectives, exchange(): return lax.all_to_all(value, axis, 0, 0, tiled=False)  55.2 us
    all_to_all x5, waiting for transfers between devices, exchange(): return lax.all_to_all(value, axis, 0, 0, tiled=False)  33.8 us
    pallas_call x11, Pallas kernels, call(): pl.pallas_call(kernel, out_shape=outs, in_specs=specs, out_specs=[vm] * l...  23.3 us
    all_to_all x5, starting transfers between devices, exchange(): return lax.all_to_all(value, axis, 0, 0, tiled=False)  23.2 us
    unnamed x25, local copies, waits for them, and re-layouts  5.61 us
  transfers between devices with their start and end apart: 5, of which 5 were waited for; matrix products, arithmetic and copies ran while one was open for 3% of the time, Pallas kernels for 0%

profile of v1, /device:TPU:0, one launch (start us, length us, event | category | flops | bytes accessed | tf_op | source)
XLA Modules:
  0.0 142.8 jit_solution(15583357528665714230)
XLA Ops:
  0.0 0.8 copy.16.gain_ref
  0.8 0.8 copy-done.2
  1.5 0.7 copy-done.4
  2.2 1.4 start_kernel.1
  3.6 8.2 %all-to-all-start = ((bf16[16,48,128]{2,1,0:T(8,128)(2,1)}), bf16[16,48,128]{2,1,0:T(8,128)(2,1)S(1)}, u32[]{:S(2)}, u32[]{:S(2)}) async-start(bf16[16,48,128]{2,1,0:T(8,128)(2,1)} %get-tuple-element.10), calls=%async_computation | async-start | bytes 393216 | tf_op jit(solution)/shard_map/all_to_all | solution.py:328
  11.7 0.0 copy-start.6
  11.7 1.3 copy.17.w_ref
  13.1 0.0 copy-done.8
  13.1 0.0 copy-start.9
  13.1 0.0 copy-start.3
  13.1 0.0 copy-start.5
  13.1 6.8 %all-to-all-done.in_ref = bf16[16,48,128]{2,1,0:T(8,128)(2,1)S(1)} async-done(((bf16[16,48,128]{2,1,0:T(8,128)(2,1)}), bf16[16,48,128]{2,1,0:T(8,128)(2,1)S(1)}, u32[]{:S(2)}, u32[]{:S(2)}) %all-to-all-start) | async-done | bytes 196640 | tf_op jit(solution)/shard_map/all_to_all | solution.py:328
  19.9 1.0 qkv_kernel.1
  20.9 4.3 %all-to-all-start.1 = ((bf16[8,16,512]{2,1,0:T(8,128)(2,1)}), bf16[8,16,512]{2,1,0:T(8,128)(2,1)S(1)}, u32[]{:S(2)}, u32[]{:S(2)}) async-start(bf16[8,16,512]{2,1,0:T(8,128)(2,1)} %qkv_kernel.1), calls=%async_computation.1 | async-start | bytes 262144 | tf_op jit(solution)/shard_map/all_to_all | solution.py:328
  25.2 0.0 copy-done.6
  25.2 0.1 add_convert_fusion
  25.3 6.0 %all-to-all-done.1.in_ref = bf16[8,16,512]{2,1,0:T(8,128)(2,1)S(1)} async-done(((bf16[8,16,512]{2,1,0:T(8,128)(2,1)}), bf16[8,16,512]{2,1,0:T(8,128)(2,1)S(1)}, u32[]{:S(2)}, u32[]{:S(2)}) %all-to-all-start.1) | async-done | bytes 131104 | tf_op jit(solution)/shard_map/all_to_all | solution.py:328
  31.3 0.9 qkv_sum_kernel.1
  32.2 3.6 %all-to-all-start.2 = ((bf16[16,16,512]{2,1,0:T(8,128)(2,1)}), bf16[16,16,512]{2,1,0:T(8,128)(2,1)S(1)}, u32[]{:S(2)}, u32[]{:S(2)}) async-start(bf16[16,16,512]{2,1,0:T(8,128)(2,1)} %qkv_sum_kernel.1), calls=%async_computation.2 | async-start | bytes 524288 | tf_op jit(solution)/shard_map/all_to_all | solution.py:328
  35.9 0.0 copy-done.9
  35.9 0.5 fusion
  36.4 8.0 %all-to-all-done.2.in_ref = bf16[16,16,512]{2,1,0:T(8,128)(2,1)S(1)} async-done(((bf16[16,16,512]{2,1,0:T(8,128)(2,1)}), bf16[16,16,512]{2,1,0:T(8,128)(2,1)S(1)}, u32[]{:S(2)}, u32[]{:S(2)}) %all-to-all-start.2) | async-done | bytes 262176 | tf_op jit(solution)/shard_map/all_to_all | solution.py:328
  44.4 0.0 copy-done.3
  44.4 0.0 copy-done.5
  44.4 15.5 %attend_kernel.1 = bf16[16,4,32,128]{3,2,1,0:T(8,128)(2,1)S(1)} custom-call(s32[32]{0:T(128)S(1)} %copy-done.5, s32[32]{0:T(128)S(1)} %copy-done.6, s32[32,128]{1,0:T(8,128)S(1)} %copy-done.3, bf16[16,16,512]{2,1,0:T(8,128)(2,1)S(1)} %all-to-all-done.2.in_ref, f32[32,4,128]{2,1,0:T(4,128)S(1)} %get-tuple-element.16.cos_ref, ...), custom_call_target="tpu_custom_call" | custom-call | tf_op jit(solution)/shard_map/attend_kernel/pallas_call | solution.py:52
  59.9 0.0 copy-start.1
  59.9 13.9 %all_to_all.50.in_ref = bf16[16,4,32,128]{3,2,1,0:T(8,128)(2,1)S(1)} all-to-all(bf16[16,4,32,128]{3,2,1,0:T(8,128)(2,1)S(1)} %attend_kernel.1), channel_id=1, replica_groups=mesh['grp'=8,'seq'=16] {'seq'}, dimensions={0} | all-to-all | bytes 1048576 | tf_op jit(solution)/shard_map/all_to_all | solution.py:328
  73.8 0.7 merge_kernel.1
  74.5 8.2 %all_to_all.51.in_ref = bf16[8,16,384]{2,1,0:T(8,128)(2,1)S(1)} all-to-all(bf16[8,16,384]{2,1,0:T(8,128)(2,1)S(1)} %merge_kernel.1), channel_id=1, replica_groups=mesh['grp'=8,'seq'=16] {'grp'}, dimensions={0} | all-to-all | bytes 196608 | tf_op jit(solution)/shard_map/all_to_all | solution.py:328
  82.7 0.0 copy-done.1
  82.7 1.0 project_kernel.2
  83.7 3.5 %all-to-all-start.5 = ((bf16[16,40,128]{2,1,0:T(8,128)(2,1)}), bf16[16,40,128]{2,1,0:T(8,128)(2,1)S(1)}, u32[]{:S(2)}, u32[]{:S(2)}) async-start(bf16[16,40,128]{2,1,0:T(8,128)(2,1)} %project_kernel.2), calls=%async_computation.5 | async-start | bytes 327680 | tf_op jit(solution)/shard_map/all_to_all | solution.py:328
  87.2 0.1 copy.18.gain_ref
  87.3 7.8 %all-to-all-done.5.in_ref = bf16[16,40,128]{2,1,0:T(8,128)(2,1)S(1)} async-done(((bf16[16,40,128]{2,1,0:T(8,128)(2,1)}), bf16[16,40,128]{2,1,0:T(8,128)(2,1)S(1)}, u32[]{:S(2)}, u32[]{:S(2)}) %all-to-all-start.5) | async-done | bytes 163872 | tf_op jit(solution)/shard_map/all_to_all | solution.py:328
  95.1 0.8 middle_kernel.1
  95.9 3.6 %all-to-all-start.6 = ((bf16[16,48,128]{2,1,0:T(8,128)(2,1)}), bf16[16,48,128]{2,1,0:T(8,128)(2,1)S(1)}, u32[]{:S(2)}, u32[]{:S(2)}) async-start(bf16[16,48,128]{2,1,0:T(8,128)(2,1)} %get-tuple-element.12), calls=%async_computation.6 | async-start | bytes 393216 | tf_op jit(solution)/shard_map/all_to_all | solution.py:328
  99.5 0.0 copy-done.7
  99.5 1.1 copy.19.gate_ref
  100.7 1.8 %copy.20.up_ref = bf16[640,864]{1,0:T(8,128)(2,1)S(1)} copy(bf16[640,864]{0,1:T(8,128)(2,1)} %param.27) | data formatting | bytes 2211840 | tf_op args[12]
  102.4 5.2 %all-to-all-done.6.in_ref = bf16[16,48,128]{2,1,0:T(8,128)(2,1)S(1)} async-done(((bf16[16,48,128]{2,1,0:T(8,128)(2,1)}), bf16[16,48,128]{2,1,0:T(8,128)(2,1)S(1)}, u32[]{:S(2)}, u32[]{:S(2)}) %all-to-all-start.6) | async-done | bytes 196640 | tf_op jit(solution)/shard_map/all_to_all | solution.py:328
  107.6 0.6 gate_kernel.1
  108.3 0.0 copy-start
  108.3 12.1 %all_to_all.52.in_ref = bf16[8,16,1792]{2,1,0:T(8,128)(2,1)S(1)} all-to-all(bf16[8,16,1792]{2,1,0:T(8,128)(2,1)S(1)} %gate_kernel.1), channel_id=1, replica_groups=mesh['grp'=8,'seq'=16] {'grp'}, dimensions={0} | all-to-all | bytes 917504 | tf_op jit(solution)/shard_map/all_to_all | solution.py:328
  120.4 0.2 hidden_kernel.1
  120.6 9.6 %all_to_all.53.in_ref = bf16[8,16,896]{2,1,0:T(8,128)(2,1)S(1)} all-to-all(bf16[8,16,896]{2,1,0:T(8,128)(2,1)S(1)} %hidden_kernel.1), channel_id=1, replica_groups=mesh['grp'=8,'seq'=16] {'grp'}, dimensions={0} | all-to-all | bytes 458752 | tf_op jit(solution)/shard_map/all_to_all | solution.py:328
  130.2 0.4 project_kernel.3
  130.6 11.5 %all_to_all.54.in_ref = bf16[16,40,128]{2,1,0:T(8,128)(2,1)S(1)} all-to-all(bf16[16,40,128]{2,1,0:T(8,128)(2,1)S(1)} %project_kernel.3), channel_id=1, replica_groups=mesh['grp'=8,'seq'=16] {'seq'}, dimensions={0} | all-to-all | bytes 327680 | tf_op jit(solution)/shard_map/all_to_all | solution.py:328
  142.1 0.8 finish_kernel.1
  (9 shorter events, 0.0 us)
Async XLA Ops:
  0.0 13.1 %copy-start.8 = (f32[448]{0:T(512)S(1)}, f32[448]{0:T(512)}, u32[]{:S(2)}) copy-start(f32[448]{0:T(512)} %param.23) | copy-start | bytes 5380
  0.8 0.8 copy-start.2
  1.5 0.7 copy-start.4
  3.6 16.3 %all-to-all-start = ((bf16[16,48,128]{2,1,0:T(8,128)(2,1)}), bf16[16,48,128]{2,1,0:T(8,128)(2,1)S(1)}, u32[]{:S(2)}, u32[]{:S(2)}) async-start(bf16[16,48,128]{2,1,0:T(8,128)(2,1)} %get-tuple-element.10), calls=%async_computation | async-start | bytes 393216 | tf_op jit(solution)/shard_map/all_to_all | solution.py:328
  11.7 13.4 %copy-start.6 = (s32[32]{0:T(128)S(1)}, s32[32]{0:T(128)}, u32[]{:S(2)}) copy-start(s32[32]{0:T(128)} %len_ref.1) | copy-start | bytes 388
  13.1 22.8 %copy-start.9 = (f32[128]{0:T(128)S(1)}, f32[128]{0:T(128)}, u32[]{:S(2)}) copy-start(f32[128]{0:T(128)} %constant.11.clone) | copy-start | bytes 1540
  13.1 31.3 %copy-start.3 = (s32[32,128]{1,0:T(8,128)S(1)}, s32[32,128]{1,0:T(8,128)}, u32[]{:S(2)}) copy-start(s32[32,128]{1,0:T(8,128)} %page_ref.1) | copy-start | bytes 49156
  13.1 31.3 %copy-start.5 = (s32[32]{0:T(128)S(1)}, s32[32]{0:T(128)}, u32[]{:S(2)}) copy-start(s32[32]{0:T(128)} %perm_ref.3) | copy-start | bytes 388
  20.9 10.4 %all-to-all-start.1 = ((bf16[8,16,512]{2,1,0:T(8,128)(2,1)}), bf16[8,16,512]{2,1,0:T(8,128)(2,1)S(1)}, u32[]{:S(2)}, u32[]{:S(2)}) async-start(bf16[8,16,512]{2,1,0:T(8,128)(2,1)} %qkv_kernel.1), calls=%async_computation.1 | async-start | bytes 262144 | tf_op jit(solution)/shard_map/all_to_all | solution.py:328
  32.2 12.1 %all-to-all-start.2 = ((bf16[16,16,512]{2,1,0:T(8,128)(2,1)}), bf16[16,16,512]{2,1,0:T(8,128)(2,1)S(1)}, u32[]{:S(2)}, u32[]{:S(2)}) async-start(bf16[16,16,512]{2,1,0:T(8,128)(2,1)} %qkv_sum_kernel.1), calls=%async_computation.2 | async-start | bytes 524288 | tf_op jit(solution)/shard_map/all_to_all | solution.py:328
  59.9 22.8 %copy-start.1 = (bf16[320,640]{1,0:T(8,128)(2,1)S(1)}, bf16[320,640]{1,0:T(8,128)(2,1)}, u32[]{:S(2)}) copy-start(bf16[320,640]{1,0:T(8,128)(2,1)} %w_ref.3) | copy-start | bytes 1228804
  73.8 13.4 %copy-start.10 = (f32[40]{0:T(128)S(1)}, f32[40]{0:T(128)}, u32[]{:S(2)}) copy-start(f32[40]{0:T(128)} %param.25) | copy-start | bytes 484
  73.8 25.8 %copy-start.7 = (bf16[640,864]{0,1:T(8,128)(2,1)S(1)}, bf16[640,864]{0,1:T(8,128)(2,1)}, u32[]{:S(2)}) copy-start(bf16[640,864]{0,1:T(8,128)(2,1)} %param.26) | copy-start | bytes 3317764
  83.7 11.5 %all-to-all-start.5 = ((bf16[16,40,128]{2,1,0:T(8,128)(2,1)}), bf16[16,40,128]{2,1,0:T(8,128)(2,1)S(1)}, u32[]{:S(2)}, u32[]{:S(2)}) async-start(bf16[16,40,128]{2,1,0:T(8,128)(2,1)} %project_kernel.2), calls=%async_computation.5 | async-start | bytes 327680 | tf_op jit(solution)/shard_map/all_to_all | solution.py:328
  95.9 11.7 %all-to-all-start.6 = ((bf16[16,48,128]{2,1,0:T(8,128)(2,1)}), bf16[16,48,128]{2,1,0:T(8,128)(2,1)S(1)}, u32[]{:S(2)}, u32[]{:S(2)}) async-start(bf16[16,48,128]{2,1,0:T(8,128)(2,1)} %get-tuple-element.12), calls=%async_computation.6 | async-start | bytes 393216 | tf_op jit(solution)/shard_map/all_to_all | solution.py:328
  108.3 21.9 %copy-start = (bf16[864,640]{1,0:T(8,128)(2,1)S(1)}, bf16[864,640]{1,0:T(8,128)(2,1)}, u32[]{:S(2)}) copy-start(bf16[864,640]{1,0:T(8,128)(2,1)} %w_ref.4) | copy-start | bytes 3317764

commit v2 on v1

--- a/solution.py
+++ b/solution.py
@@ -13,6 +13,7 @@
 KV_HEADS = 8
 HEAD_DIM = 128
 STEPS = 4
+AHEAD = 2
 REQ_GRP = 4
 SHARD_PAGES = 8
 PAGE = 128
@@ -21,6 +22,7 @@
 GROUP_ROWS = REQ_GRP * STEPS
 N_GRP = 8
 N_SEQ = 16
+N_CHIP = N_GRP // 2
 FEAT = D // (N_GRP * N_SEQ)
 FEAT_PAD = 48
 GFEAT = D // N_GRP
@@ -44,9 +46,10 @@
         if i in smem:
             specs.append(pl.BlockSpec(memory_space=pltpu.SMEM))
         elif i in anys:
-            specs.append(pl.BlockSpec(memory_space=pl.ANY))
+            specs.append(pl.BlockSpec(memory_space=pltpu.HBM))
         else:
             specs.append(pl.BlockSpec(memory_space=pltpu.VMEM))
+    args = [pltpu.with_memory_space_constraint(v, pltpu.HBM) if i in anys else v for i, v in enumerate(args)]
     many = isinstance(outs, (list, tuple))
     vm = pl.BlockSpec(memory_space=pltpu.VMEM)
     return pl.pallas_call(
@@ -56,7 +59,7 @@
         out_specs=[vm] * len(outs) if many else vm,
         scratch_shapes=list(scratch),
         name=getattr(kernel, "__name__", "kernel"),
-        compiler_params=pltpu.CompilerParams(vmem_limit_bytes=48 << 20),
+        compiler_params=pltpu.CompilerParams(vmem_limit_bytes=32 << 20),
     )(*args)
 
 
@@ -81,17 +84,29 @@
         out_ref[s] = block
 
 
-def start_kernel(perm_ref, tok_ref, gain_ref, send_ref, xt_ref, hot_ref):
+def start_kernel(perm_hbm, tok_hbm, gain_hbm, send_ref, xt_ref, hot_ref, perm_ref, tok_ref, gain_ref, sems):
+    copies = [
+        pltpu.make_async_copy(perm_hbm, perm_ref, sems.at[0]),
+        pltpu.make_async_copy(tok_hbm, tok_ref, sems.at[1]),
+        pltpu.make_async_copy(gain_hbm, gain_ref, sems.at[2]),
+    ]
+    for copy in copies:
+        copy.start()
+    for copy in copies:
+        copy.wait()
     lane = iota((8, ROWS), 1)
     source = lane & (STEPS - 1)
     for n in range(REQUESTS):
         source = source + jnp.where((lane >> 2) == n, perm_ref[n] * STEPS, 0)
     hot = jnp.where(iota((ROWS, ROWS), 0) == source[0:1, :], 1.0, 0.0).astype(BF)
     hot_ref[...] = hot
-    xt = lax.dot_general(tok_ref[...], hot, (((0,), (0,)), ((), ())), preferred_element_type=F32)
+    tok = tok_ref[...]
+    scaled = (tok.astype(F32) * gain_ref[...]).astype(BF)
+    turn = (((0,), (0,)), ((), ()))
+    xt = lax.dot_general(tok, hot, turn, preferred_element_type=F32)
     xt_ref[...] = xt
     squares = jnp.sum(xt * xt, axis=0, keepdims=True)
-    spread_features(xt * gain_ref[...], squares, send_ref)
+    spread_features(lax.dot_general(scaled, hot, turn, preferred_element_type=F32), squares, send_ref)
 
 
 def collect_features(in_ref, scratch):
@@ -138,28 +153,36 @@
 
 def attend_kernel(
     perm_ref, len_ref, page_ref, in_ref, cos_ref, sin_ref, k_hbm, v_hbm, out_ref,
-    kbuf, vbuf, qbuf, knew, vnew, rot, sems,
+    qbuf, knew, vnew, rot, sbuf, obuf, kbuf, vbuf, sems,
 ):
     grp_idx = lax.axis_index("grp")
     seq_idx = lax.axis_index("seq")
-
-    def copies(r, p):
-        slot = page_ref[perm_ref[grp_idx * REQ_GRP + r], seq_idx * SHARD_PAGES + p]
-        rows = pl.ds(p * PAGE, PAGE)
-        return (
-            pltpu.make_async_copy(k_hbm.at[slot], kbuf.at[r, rows], sems.at[r, p, 0]),
-            pltpu.make_async_copy(v_hbm.at[slot], vbuf.at[r, rows], sems.at[r, p, 1]),
-        )
-
+    members = [perm_ref[grp_idx * REQ_GRP + r] for r in range(REQ_GRP)]
+    copies = [[], []]
     for r in range(REQ_GRP):
-        for p in range(SHARD_PAGES):
-            for copy in copies(r, p):
+        for kind, (pool, buf) in enumerate(((k_hbm, kbuf), (v_hbm, vbuf))):
+            pages = []
+            for p in range(SHARD_PAGES):
+                slot = page_ref[members[r], seq_idx * SHARD_PAGES + p]
+                to = buf.at[r, pl.ds(p * PAGE, PAGE)]
+                pages.append(pltpu.make_async_copy(pool.at[slot], to, sems.at[kind, r]))
+            copies[kind].append(pages)
+
+    def begin(kind, r):
+        if r < REQ_GRP:
+            for copy in copies[kind][r]:
                 copy.start()
 
+    def await_pages(kind, r):
+        whole = (kbuf, vbuf)[kind].at[r]
+        pltpu.make_async_copy(whole, whole, sems.at[kind, r]).wait()
+
+    for r in range(AHEAD):
+        begin(0, r)
+        begin(1, r)
     for r in range(REQ_GRP):
-        member = perm_ref[grp_idx * REQ_GRP + r]
-        rot[0, r * STEPS : (r + 1) * STEPS, :] = cos_ref[member]
-        rot[1, r * STEPS : (r + 1) * STEPS, :] = sin_ref[member]
+        rot[0, r * STEPS : (r + 1) * STEPS, :] = cos_ref[members[r]]
+        rot[1, r * STEPS : (r + 1) * STEPS, :] = sin_ref[members[r]]
     cosine = rot[0]
     sine = rot[1]
     knew[...] = jnp.zeros_like(knew)
@@ -183,9 +206,9 @@
             if head < HEADS:
                 h, j = divmod(head, HEADS // KV_HEADS)
                 for r in range(REQ_GRP):
-                    qbuf[r, h * QROWS + j * STEPS : h * QROWS + (j + 1) * STEPS, :] = value[
-                        r * STEPS : (r + 1) * STEPS
-                    ]
+                    at = h * QROWS + j * STEPS
+                    side = (h % 2) * HEAD_DIM
+                    qbuf[r, at : at + STEPS, side : side + HEAD_DIM] = value[r * STEPS : (r + 1) * STEPS]
             elif head < HEADS + KV_HEADS:
                 h = head - HEADS
                 knew[:GROUP_ROWS, h * HEAD_DIM : (h + 1) * HEAD_DIM] = value.astype(BF)
@@ -194,71 +217,80 @@
                 vnew[:GROUP_ROWS, h * HEAD_DIM : (h + 1) * HEAD_DIM] = value.astype(BF)
 
     score_scale = HEAD_DIM ** (-0.5)
-    step = iota((QROWS, PAGE), 0) & (STEPS - 1)
-    column = iota((QROWS, PAGE), 1)
-    place = iota((QROWS, SHARD_KEYS), 1)
-    lane = iota((QROWS, HEAD_DIM), 1)
-    is_last = seq_idx == N_SEQ - 1
+    power = score_scale * float(np.log2(np.e))
+    step = iota((2 * QROWS, PAGE), 0) & (STEPS - 1)
+    column = iota((2 * QROWS, PAGE), 1)
+    own_live = ((column & (STEPS - 1)) <= step) & (seq_idx == N_SEQ - 1) & (column < GROUP_ROWS)
+    place = iota((8, SHARD_KEYS), 1)
+    group = iota((2 * QROWS, HEAD_DIM), 1) >> 3
+    word = lax.rem(group, 3)
+    part_lane = iota((STEPS, HEAD_DIM), 1)
     nt = (((1,), (1,)), ((), ()))
-
-    def one(r, carry):
-        for p in range(SHARD_PAGES):
-            for copy in copies(r, p):
-                copy.wait()
-        live = len_ref[perm_ref[grp_idx * REQ_GRP + r]] - seq_idx * SHARD_KEYS
-        live_mask = place < live
-        own_mask = ((column >> 2) == r) & ((column & (STEPS - 1)) <= step) & is_last & (column < GROUP_ROWS)
-        for h in range(KV_HEADS):
-            lanes = slice(h * HEAD_DIM, (h + 1) * HEAD_DIM)
-            query = qbuf[r, h * QROWS : (h + 1) * QROWS, :].astype(BF)
+    for r in range(REQ_GRP):
+        await_pages(0, r)
+        begin(0, r + AHEAD)
+        live = len_ref[members[r]] - seq_idx * SHARD_KEYS
+        bias = jnp.where(place < live, 0.0, LOW_SCORE)[0:1]
+        own_bias = jnp.where(own_live & ((column >> 2) == r), 0.0, LOW_SCORE)
+        for h in range(0, KV_HEADS, 2):
+            lanes = slice(h * HEAD_DIM, (h + 2) * HEAD_DIM)
+            rows = slice(h * QROWS, (h + 2) * QROWS)
+            query = qbuf[r, rows, :].astype(BF)
             scores = lax.dot_general(query, kbuf[r, :, lanes], nt, preferred_element_type=F32)
-            scores = jnp.where(live_mask, scores * score_scale, LOW_SCORE)
+            sbuf[rows, :SHARD_KEYS] = scores + bias
             own = lax.dot_general(query, knew[:, lanes], nt, preferred_element_type=F32)
-            own = jnp.where(own_mask, own * score_scale, LOW_SCORE)
-            best = jnp.maximum(
-                jnp.max(scores, axis=1, keepdims=True), jnp.max(own, axis=1, keepdims=True)
-            )
-            weight = jnp.where(live_mask, jnp.exp(scores - best), 0.0)
-            own_weight = jnp.where(own_mask, jnp.exp(own - best), 0.0)
-            total = jnp.sum(weight, axis=1, keepdims=True) + jnp.sum(own_weight, axis=1, keepdims=True)
-            mixed = jnp.dot(
-                weight.astype(BF), vbuf[r, :, lanes], preferred_element_type=F32
-            ) + jnp.dot(own_weight.astype(BF), vnew[:, lanes], preferred_element_type=F32)
-            some = total > 0.0
-            safe = jnp.where(some, total, 1.0)
-            mixed = mixed / safe
-            level = jnp.where(some, best + jnp.log(safe), LOW_SCORE)
-            hi, rest = split(level)
+            sbuf[rows, SHARD_KEYS:] = own + own_bias
+        await_pages(1, r)
+        begin(1, r + AHEAD)
+        for pair in range(0, KV_HEADS, 2):
+            lanes = slice(pair * HEAD_DIM, (pair + 2) * HEAD_DIM)
+            scores = sbuf[pair * QROWS : (pair + 2) * QROWS, :]
+            best = jnp.max(scores, axis=1, keepdims=True)
+            weight = jnp.exp2((scores - best) * power)
+            total = jnp.sum(weight, axis=1, keepdims=True)
+            weight = weight.astype(BF)
+            both = jnp.dot(
+                weight[:, :SHARD_KEYS], vbuf[r, :, lanes], preferred_element_type=F32
+            ) + jnp.dot(weight[:, SHARD_KEYS:], vnew[:, lanes], preferred_element_type=F32)
+            both = both / total
+            levels = jnp.where(best > 0.1 * LOW_SCORE, best * score_scale + jnp.log(total), LOW_SCORE)
+            hi, rest = split(levels)
             mid, low = split(rest)
-            level = jnp.where(lane < 32, hi, jnp.where(lane < 64, mid, low))
-            both = jnp.concatenate([mixed[:16], level[:16]], axis=0)
-            out_ref[2 * h, r] = both.astype(BF)
-            both = jnp.concatenate([mixed[8:], level[8:]], axis=0)
-            out_ref[2 * h + 1, r] = both.astype(BF)
-        return carry
-
-    lax.fori_loop(0, REQ_GRP, one, 0)
-
-
-def merge_kernel(in_ref, out_ref, scratch):
-    for r in range(REQ_GRP):
-        levels = []
+            levels = jnp.where(word == 0, hi, jnp.where(word == 1, mid, low))
+            for side in range(2):
+                h = pair + side
+                mixed = both[side * QROWS : (side + 1) * QROWS, side * HEAD_DIM : (side + 1) * HEAD_DIM]
+                level = levels[side * QROWS : (side + 1) * QROWS]
+                for half in range(2):
+                    to = slice(r * STEPS, (r + 1) * STEPS)
+                    parts = [slice((2 * half + j) * STEPS, (2 * half + j + 1) * STEPS) for j in range(3)]
+                    for j in range(3):
+                        obuf[2 * h + half, to, j * HEAD_DIM : (j + 1) * HEAD_DIM] = mixed[parts[j]]
+                    obuf[2 * h + half, to, 3 * HEAD_DIM :] = jnp.where(
+                        part_lane < 24, level[parts[0]], jnp.where(part_lane < 48, level[parts[1]], level[parts[2]])
+                    )
+    for s in range(N_SEQ):
+        out_ref[s] = obuf[s].astype(BF)
+
+
+def merge_kernel(in_ref, out_ref):
+    levels = []
+    for s in range(N_SEQ):
+        cols = in_ref[s, :, 3 * HEAD_DIM :].astype(F32)
+        levels.append(
+            [cols[:, a : a + 1] + cols[:, a + 8 : a + 9] + cols[:, a + 16 : a + 17] for a in (0, 24, 48)]
+        )
+    out = []
+    for j in range(3):
+        best = functools.reduce(jnp.maximum, [level[j] for level in levels])
+        total = jnp.zeros_like(best)
+        value = jnp.zeros((GROUP_ROWS, HEAD_DIM), F32)
         for s in range(N_SEQ):
-            cols = in_ref[s, r, 16:, :].astype(F32)
-            levels.append(cols[:, 0:1] + cols[:, 32:33] + cols[:, 64:65])
-        best = functools.reduce(jnp.maximum, levels)
-        total = jnp.zeros_like(best)
-        value = jnp.zeros((16, HEAD_DIM), F32)
-        for s in range(N_SEQ):
-            factor = jnp.exp(levels[s] - best)
+            factor = jnp.exp(levels[s][j] - best)
             total = total + factor
-            value = value + in_ref[s, r, :16, :].astype(F32) * factor
-        value = value / total
-        for j in range(3):
-            scratch[r * STEPS : (r + 1) * STEPS, j * HEAD_DIM : (j + 1) * HEAD_DIM] = value[
-                j * STEPS : (j + 1) * STEPS
-            ]
-    value = scratch[...]
+            value = value + in_ref[s, :, j * HEAD_DIM : (j + 1) * HEAD_DIM].astype(F32) * factor
+        out.append(value / total)
+    value = jnp.concatenate(out, axis=1)
     odd = lax.rem(lax.axis_index("seq"), 2) == 1
     value = jnp.where(odd, pltpu.roll(value, 3 * HEAD_DIM - HEAD_DIM // 2, 1), value).astype(BF)
     for g in range(N_GRP):
@@ -269,6 +301,14 @@
     turned = part.T
     for s in range(N_SEQ):
         out_ref[s] = turned[s * FEAT : (s + 1) * FEAT].astype(BF)
+
+
+def on_second_core():
+    return lax.rem(lax.axis_index("grp"), 2) == 1
+
+
+def on_second_core():
+    return lax.rem(lax.axis_index("grp"), 2) == 1
 
 
 def project_kernel(in_ref, w_ref, out_ref):
@@ -287,25 +327,50 @@
     spread_features(total * gain_ref[...], squares, send_ref)
 
 
-def gate_kernel(in_ref, gate_ref, up_ref, out_ref, scratch):
+def gate_kernel(in_ref, gate_ref, up_ref, keep_ref, give_ref, scratch):
     value, squares = collect_features(in_ref, scratch)
     gate = jnp.dot(value, gate_ref[...], preferred_element_type=F32)
     up = jnp.dot(value, up_ref[...], preferred_element_type=F32)
     hi, lo = split(squares)
-    for g in range(N_GRP):
-        rows = slice(g * GROUP_ROWS, (g + 1) * GROUP_ROWS)
-        out_ref[g, :, :FCOLS] = gate[rows].astype(BF)
-        out_ref[g, :, FCOLS:FPAD] = jnp.where(
-            iota((GROUP_ROWS, FPAD - FCOLS), 1) < 16, hi[rows, : FPAD - FCOLS], lo[rows, : FPAD - FCOLS]
-        ).astype(BF)
-        out_ref[g, :, FPAD : FPAD + FCOLS] = up[rows].astype(BF)
-        out_ref[g, :, FPAD + FCOLS :] = jnp.zeros((GROUP_ROWS, FPAD - FCOLS), BF)
+    tail = FPAD - FCOLS
+    sums = jnp.where(iota((ROWS, tail), 1) < tail // 2, hi[:, :tail], lo[:, :tail])
+    second = on_second_core()
+    spare = slice(FCOLS, FPAD)
+    for x in range(N_CHIP):
+        first_rows = slice(2 * x * GROUP_ROWS, (2 * x + 1) * GROUP_ROWS)
+        last_rows = slice((2 * x + 1) * GROUP_ROWS, (2 * x + 2) * GROUP_ROWS)
+        for lanes, part in (
+            (slice(0, FCOLS), gate),
+            (spare, sums),
+            (slice(FPAD, FPAD + FCOLS), up),
+        ):
+            first = part[first_rows]
+            last = part[last_rows]
+            keep_ref[x, :, lanes] = jnp.where(second, last, first)
+            give_ref[x, :, lanes] = jnp.where(second, first, last).astype(BF)
+        keep_ref[x, :, FPAD + FCOLS :] = jnp.zeros((GROUP_ROWS, tail), F32)
+        give_ref[x, :, FPAD + FCOLS :] = jnp.zeros((GROUP_ROWS, tail), BF)
+
+
+def pair_kernel(keep_ref, got_ref, out_ref):
+    tail = (FPAD - FCOLS) // 2
+    start = FPAD - 128
+    lane = iota((GROUP_ROWS, 128), 1)
+    for x in range(N_CHIP):
+        total = keep_ref[x] + got_ref[x].astype(F32)
+        out_ref[x] = total.astype(BF)
+        last = total[:, start:FPAD]
+        hi, lo = split(last + pltpu.roll(last, 128 - tail, 1))
+        last = jnp.where(
+            lane < 128 - 2 * tail, last, jnp.where(lane < 128 - tail, hi, pltpu.roll(lo, tail, 1))
+        )
+        out_ref[x, :, start:FPAD] = last.astype(BF)
 
 
 def hidden_kernel(in_ref, out_ref):
     total = in_ref[0].astype(F32)
-    for g in range(1, N_GRP):
-        total = total + in_ref[g].astype(F32)
+    for x in range(1, N_CHIP):
+        total = total + in_ref[x].astype(F32)
     scale = scale_of(total, FCOLS)
     gate = total[:, :FPAD] * scale
     up = total[:, FPAD:] * scale
@@ -326,6 +391,15 @@
 
 def exchange(value, axis):
     return lax.all_to_all(value, axis, 0, 0, tiled=False)
+
+
+def exchange_chips(value):
+    groups = [list(range(core, N_GRP, 2)) for core in range(2)]
+    return lax.all_to_all(value, "grp", 0, 0, axis_index_groups=groups, tiled=False)
+
+
+def swap_cores(value):
+    return lax.ppermute(value, "grp", [(i, i ^ 1) for i in range(N_GRP)])
 
 
 def body(
@@ -343,8 +417,14 @@
     send, xt, hot = call(
         start_kernel,
         [sds((N_SEQ, FEAT_PAD, ROWS)), sds((FEAT, ROWS), F32), sds((ROWS, ROWS))],
-        group_perm, tokens.reshape(ROWS, FEAT), gain_in[:, None],
-        smem=(0,),
+        group_perm, tokens.reshape(ROWS, FEAT), gain_in[None, :],
+        anys=(0, 1, 2),
+        scratch=[
+            pltpu.SMEM((REQUESTS,), jnp.int32),
+            pltpu.VMEM((ROWS, FEAT), BF),
+            pltpu.VMEM((1, FEAT), F32),
+            pltpu.SemaphoreType.DMA((3,)),
+        ],
     )
     got = exchange(send, "seq")
     send = call(
@@ -356,24 +436,23 @@
     send = call(qkv_sum_kernel, sds((N_SEQ, GROUP_ROWS, QPAD)), got, bias)
     got = exchange(send, "seq")
     send = call(
-        attend_kernel, sds((N_SEQ, REQ_GRP, 32, HEAD_DIM)),
+        attend_kernel, sds((N_SEQ, GROUP_ROWS, 4 * HEAD_DIM)),
         group_perm, lengths, page_table, got, cosine, sine, k_pool, v_pool,
         smem=(0, 1, 2), anys=(6, 7),
         scratch=[
-            pltpu.VMEM((REQ_GRP, SHARD_KEYS, KV_HEADS * HEAD_DIM), BF),
-            pltpu.VMEM((REQ_GRP, SHARD_KEYS, KV_HEADS * HEAD_DIM), BF),
-            pltpu.VMEM((REQ_GRP, KV_HEADS * QROWS, HEAD_DIM), F32),
+            pltpu.VMEM((REQ_GRP, KV_HEADS * QROWS, 2 * HEAD_DIM), F32),
             pltpu.VMEM((PAGE, KV_HEADS * HEAD_DIM), BF),
             pltpu.VMEM((PAGE, KV_HEADS * HEAD_DIM), BF),
             pltpu.VMEM((2, GROUP_ROWS, HEAD_DIM), F32),
-            pltpu.SemaphoreType.DMA((REQ_GRP, SHARD_PAGES, 2)),
+            pltpu.VMEM((KV_HEADS * QROWS, SHARD_KEYS + PAGE), F32),
+            pltpu.VMEM((N_SEQ, GROUP_ROWS, 4 * HEAD_DIM), F32),
+            pltpu.VMEM((REQ_GRP, SHARD_KEYS, KV_HEADS * HEAD_DIM), BF),
+            pltpu.VMEM((REQ_GRP, SHARD_KEYS, KV_HEADS * HEAD_DIM), BF),
+            pltpu.SemaphoreType.DMA((2, REQ_GRP)),
         ],
     )
     got = exchange(send, "seq")
-    send = call(
-        merge_kernel, sds((N_GRP, GROUP_ROWS, 3 * HEAD_DIM)), got,
-        scratch=[pltpu.VMEM((GROUP_ROWS, 3 * HEAD_DIM), F32)],
-    )
+    send = call(merge_kernel, sds((N_GRP, GROUP_ROWS, 3 * HEAD_DIM)), got)
     got = exchange(send, "grp")
     send = call(project_kernel, sds((N_SEQ, FEAT, ROWS)), got, o_weight)
     got = exchange(send, "seq")
@@ -382,11 +461,14 @@
         got, xt, gain_mid[:, None],
     )
     got = exchange(send, "seq")
-    send = call(
-        gate_kernel, sds((N_GRP, GROUP_ROWS, 2 * FPAD)), got, gate_weight, up_weight,
+    keep, give = call(
+        gate_kernel,
+        [sds((N_CHIP, GROUP_ROWS, 2 * FPAD), F32), sds((N_CHIP, GROUP_ROWS, 2 * FPAD))],
+        got, gate_weight, up_weight,
         scratch=[pltpu.VMEM((GFEAT, ROWS), F32)],
     )
-    got = exchange(send, "grp")
+    send = call(pair_kernel, sds((N_CHIP, GROUP_ROWS, 2 * FPAD)), keep, swap_cores(give))
+    got = exchange_chips(send)
     send = call(hidden_kernel, sds((N_GRP, GROUP_ROWS, FPAD)), got)
     got = exchange(send, "grp")
     send = call(project_kernel, sds((N_SEQ, FEAT, ROWS)), got, down_weight)

time: 144 us -> 132 us (0.917)
  Pallas kernels: 23.3 us -> 16.2 us
  blocking collectives: 55.2 us -> 50.6 us
  local copies, waits for them, and re-layouts: 6.46 us -> 4.3 us
  waiting for transfers between devices: 33.8 us -> 35.3 us
    all_to_all x5 -> x4, blocking collectives: 55.2 us -> 41.2 us  [exchange(): return lax.all_to_all(value, axis, 0, 0, tiled=False)]
    all_to_all x0 -> x1, blocking collectives: none -> 9.39 us  [exchange_chips(): lax.all_to_all(value, 'grp', 0, 0, axis_index_groups=groups, tiled=False)]
    pallas_call x11 -> x12, Pallas kernels: 23.3 us -> 16.2 us  [call(): pl.pallas_call(kernel, out_shape=outs, in_specs=specs, out_specs=[vm] * l...]
    ppermute x0 -> x1, waiting for transfers between devices: none -> 1.48 us  [swap_cores(): return lax.ppermute(value, 'grp', [(i, i ^ 1) for i in range(N_GRP)])]
    unnamed x25 -> x21, local copies, waits for them, and re-layouts: 5.61 us -> 4.2 us
  transfers between devices with their start and end apart: 5 -> 6, of which waited for: 5 -> 6; matrix products, arithmetic and copies ran while one was open for 3% -> 4% of each run, Pallas kernels for 0% -> 0%
where the time goes in v2:
time: 132 us; the launch traced here: 131 us
  blocking collectives  50.6 us (38%)
  waiting for transfers between devices  35.3 us (27%)
  starting transfers between devices  23.5 us (18%)
  Pallas kernels  16.2 us (12%)
  local copies, waits for them, and re-layouts  4.3 us (3%)
    all_to_all x4, blocking collectives, exchange(): return lax.all_to_all(value, axis, 0, 0, tiled=False)  41.2 us
    all_to_all x5, waiting for transfers between devices, exchange(): return lax.all_to_all(value, axis, 0, 0, tiled=False)  33.8 us
    all_to_all x5, starting transfers between devices, exchange(): return lax.all_to_all(value, axis, 0, 0, tiled=False)  23.4 us
    pallas_call x12, Pallas kernels, call(): pl.pallas_call(kernel, out_shape=outs, in_specs=specs, out_specs=[vm] * l...  16.2 us
    all_to_all x1, blocking collectives, exchange_chips(): lax.all_to_all(value, 'grp', 0, 0, axis_index_groups=groups, tiled=False)  9.39 us
    unnamed x21, local copies, waits for them, and re-layouts  4.2 us
  transfers between devices with their start and end apart: 6, of which 6 were waited for; matrix products, arithmetic and copies ran while one was open for 4% of the time, Pallas kernels for 0%

profile of v2, /device:TPU:0, one launch (start us, length us, event | category | flops | bytes accessed | tf_op | source)
XLA Modules:
  0.0 130.7 jit_solution(15867620312347727632)
XLA Ops:
  0.0 1.7 %start_kernel.1 = (bf16[16,48,128]{2,1,0:T(8,128)(2,1)}, f32[40,128]{1,0:T(8,128)S(1)}, bf16[128,128]{1,0:T(8,128)(2,1)S(1)}) custom-call(s32[32]{0:T(128)} %perm_ref.1, bf16[128,40]{1,0:T(8,128)(2,1)} %bitcast.6, f32[1,40]{1,0:T(1,128)} %bitcast.7), custom_call_target="tpu_custom_call" | custom-call | tf_op jit(solution)/shard_map/start_kernel/pallas_call | solution.py:55
  1.7 8.2 %all-to-all-start = ((bf16[16,48,128]{2,1,0:T(8,128)(2,1)}), bf16[16,48,128]{2,1,0:T(8,128)(2,1)S(1)}, u32[]{:S(2)}, u32[]{:S(2)}) async-start(bf16[16,48,128]{2,1,0:T(8,128)(2,1)} %get-tuple-element.12), calls=%async_computation | async-start | bytes 393216 | tf_op jit(solution)/shard_map/all_to_all | solution.py:393
  9.9 0.0 copy-start.4
  9.9 1.3 copy.16.w_ref
  11.2 0.0 copy-done.6
  11.2 0.0 copy-start.7
  11.2 0.0 copy-start.2
  11.2 0.0 copy-start.3
  11.3 6.8 %all-to-all-done.in_ref = bf16[16,48,128]{2,1,0:T(8,128)(2,1)S(1)} async-done(((bf16[16,48,128]{2,1,0:T(8,128)(2,1)}), bf16[16,48,128]{2,1,0:T(8,128)(2,1)S(1)}, u32[]{:S(2)}, u32[]{:S(2)}) %all-to-all-start) | async-done | bytes 196640 | tf_op jit(solution)/shard_map/all_to_all | solution.py:393
  18.0 1.0 qkv_kernel.1
  19.0 4.3 %all-to-all-start.1 = ((bf16[8,16,512]{2,1,0:T(8,128)(2,1)}), bf16[8,16,512]{2,1,0:T(8,128)(2,1)S(1)}, u32[]{:S(2)}, u32[]{:S(2)}) async-start(bf16[8,16,512]{2,1,0:T(8,128)(2,1)} %qkv_kernel.1), calls=%async_computation.1 | async-start | bytes 262144 | tf_op jit(solution)/shard_map/all_to_all | solution.py:393
  23.3 0.0 copy-done.4
  23.3 0.1 add_convert_fusion
  23.4 6.0 %all-to-all-done.1.in_ref = bf16[8,16,512]{2,1,0:T(8,128)(2,1)S(1)} async-done(((bf16[8,16,512]{2,1,0:T(8,128)(2,1)}), bf16[8,16,512]{2,1,0:T(8,128)(2,1)S(1)}, u32[]{:S(2)}, u32[]{:S(2)}) %all-to-all-start.1) | async-done | bytes 131104 | tf_op jit(solution)/shard_map/all_to_all | solution.py:393
  29.4 0.9 qkv_sum_kernel.1
  30.4 3.6 %all-to-all-start.2 = ((bf16[16,16,512]{2,1,0:T(8,128)(2,1)}), bf16[16,16,512]{2,1,0:T(8,128)(2,1)S(1)}, u32[]{:S(2)}, u32[]{:S(2)}) async-start(bf16[16,16,512]{2,1,0:T(8,128)(2,1)} %qkv_sum_kernel.1), calls=%async_computation.2 | async-start | bytes 524288 | tf_op jit(solution)/shard_map/all_to_all | solution.py:393
  34.0 0.0 copy-done.7
  34.0 0.5 fusion
  34.6 8.0 %all-to-all-done.2.in_ref = bf16[16,16,512]{2,1,0:T(8,128)(2,1)S(1)} async-done(((bf16[16,16,512]{2,1,0:T(8,128)(2,1)}), bf16[16,16,512]{2,1,0:T(8,128)(2,1)S(1)}, u32[]{:S(2)}, u32[]{:S(2)}) %all-to-all-start.2) | async-done | bytes 262176 | tf_op jit(solution)/shard_map/all_to_all | solution.py:393
  42.5 0.0 copy-done.2
  42.5 0.0 copy-done.3
  42.5 8.3 %attend_kernel.1 = bf16[16,16,512]{2,1,0:T(8,128)(2,1)S(1)} custom-call(s32[32]{0:T(128)S(1)} %copy-done.3, s32[32]{0:T(128)S(1)} %copy-done.4, s32[32,128]{1,0:T(8,128)S(1)} %copy-done.2, bf16[16,16,512]{2,1,0:T(8,128)(2,1)S(1)} %all-to-all-done.2.in_ref, f32[32,4,128]{2,1,0:T(4,128)S(1)} %get-tuple-element.20.cos_ref, ...), custom_call_target="tpu_custom_call" | custom-call | tf_op jit(solution)/shard_map/attend_kernel/pallas_call | solution.py:55
  50.8 0.0 copy-start.1
  50.8 0.0 copy-start.8
  50.8 12.0 %all_to_all.50.in_ref = bf16[16,16,512]{2,1,0:T(8,128)(2,1)S(1)} all-to-all(bf16[16,16,512]{2,1,0:T(8,128)(2,1)S(1)} %attend_kernel.1), channel_id=1, replica_groups=mesh['grp'=8,'seq'=16] {'seq'}, dimensions={0} | all-to-all | bytes 524288 | tf_op jit(solution)/shard_map/all_to_all | solution.py:393
  62.9 0.4 merge_kernel.1
  63.2 8.2 %all_to_all.51.in_ref = bf16[8,16,384]{2,1,0:T(8,128)(2,1)S(1)} all-to-all(bf16[8,16,384]{2,1,0:T(8,128)(2,1)S(1)} %merge_kernel.1), channel_id=1, replica_groups=mesh['grp'=8,'seq'=16] {'grp'}, dimensions={0} | all-to-all | bytes 196608 | tf_op jit(solution)/shard_map/all_to_all | solution.py:393
  71.4 0.0 copy-done.1
  71.4 1.0 project_kernel.2
  72.4 3.7 %all-to-all-start.5 = ((bf16[16,40,128]{2,1,0:T(8,128)(2,1)}), bf16[16,40,128]{2,1,0:T(8,128)(2,1)S(1)}, u32[]{:S(2)}, u32[]{:S(2)}) async-start(bf16[16,40,128]{2,1,0:T(8,128)(2,1)} %project_kernel.2), calls=%async_computation.5 | async-start | bytes 327680 | tf_op jit(solution)/shard_map/all_to_all | solution.py:393
  76.1 0.1 copy.17.gain_ref
  76.2 7.9 %all-to-all-done.5.in_ref = bf16[16,40,128]{2,1,0:T(8,128)(2,1)S(1)} async-done(((bf16[16,40,128]{2,1,0:T(8,128)(2,1)}), bf16[16,40,128]{2,1,0:T(8,128)(2,1)S(1)}, u32[]{:S(2)}, u32[]{:S(2)}) %all-to-all-start.5) | async-done | bytes 163872 | tf_op jit(solution)/shard_map/all_to_all | solution.py:393
  84.1 0.8 middle_kernel.1
  84.8 3.6 %all-to-all-start.6 = ((bf16[16,48,128]{2,1,0:T(8,128)(2,1)}), bf16[16,48,128]{2,1,0:T(8,128)(2,1)S(1)}, u32[]{:S(2)}, u32[]{:S(2)}) async-start(bf16[16,48,128]{2,1,0:T(8,128)(2,1)} %get-tuple-element.14), calls=%async_computation.6 | async-start | bytes 393216 | tf_op jit(solution)/shard_map/all_to_all | solution.py:393
  88.5 0.0 copy-done.5
  88.5 1.1 copy.18.gate_ref
  89.6 1.8 %copy.19.up_ref = bf16[640,864]{1,0:T(8,128)(2,1)S(1)} copy(bf16[640,864]{0,1:T(8,128)(2,1)} %param.27) | data formatting | bytes 2211840 | tf_op args[12]
  91.3 5.2 %all-to-all-done.6.in_ref = bf16[16,48,128]{2,1,0:T(8,128)(2,1)S(1)} async-done(((bf16[16,48,128]{2,1,0:T(8,128)(2,1)}), bf16[16,48,128]{2,1,0:T(8,128)(2,1)S(1)}, u32[]{:S(2)}, u32[]{:S(2)}) %all-to-all-start.6) | async-done | bytes 196640 | tf_op jit(solution)/shard_map/all_to_all | solution.py:393
  96.5 0.6 gate_kernel.1
  97.2 0.1 collective-permute-start
  97.3 1.5 %collective-permute-done.got_ref = bf16[4,16,1792]{2,1,0:T(8,128)(2,1)S(1)} collective-permute-done((bf16[4,16,1792]{2,1,0:T(8,128)(2,1)S(1)}, bf16[4,16,1792]{2,1,0:T(8,128)(2,1)S(1)}, u32[]{:S(2)}, u32[]{:S(2)}) %collective-permute-start) | collective-permute-done | bytes 229408 | tf_op jit(solution)/shard_map/ppermute | solution.py:402
  98.7 0.2 pair_kernel.1
  98.9 9.4 %all_to_all.52.in_ref = bf16[4,16,1792]{2,1,0:T(8,128)(2,1)S(1)} all-to-all(bf16[4,16,1792]{2,1,0:T(8,128)(2,1)S(1)} %pair_kernel.1), channel_id=1, replica_groups={{0,32,64,96},{16,48,80,112},{1,33,65,97},{17,49,81,113},{2,34,66,98},{1..., dimensions={0} | all-to-all | bytes 458752 | tf_op jit(solution)/shard_map/all_to_all | solution.py:398
  108.3 0.2 hidden_kernel.1
  108.5 9.6 %all_to_all.53.in_ref = bf16[8,16,896]{2,1,0:T(8,128)(2,1)S(1)} all-to-all(bf16[8,16,896]{2,1,0:T(8,128)(2,1)S(1)} %hidden_kernel.1), channel_id=1, replica_groups=mesh['grp'=8,'seq'=16] {'grp'}, dimensions={0} | all-to-all | bytes 458752 | tf_op jit(solution)/shard_map/all_to_all | solution.py:393
  118.1 0.4 project_kernel.3
  118.5 11.5 %all_to_all.54.in_ref = bf16[16,40,128]{2,1,0:T(8,128)(2,1)S(1)} all-to-all(bf16[16,40,128]{2,1,0:T(8,128)(2,1)S(1)} %project_kernel.3), channel_id=1, replica_groups=mesh['grp'=8,'seq'=16] {'seq'}, dimensions={0} | all-to-all | bytes 327680 | tf_op jit(solution)/shard_map/all_to_all | solution.py:393
  130.0 0.8 finish_kernel.1
  (7 shorter events, 0.0 us)
Async XLA Ops:
  0.0 11.2 %copy-start.6 = (f32[448]{0:T(512)S(1)}, f32[448]{0:T(512)}, u32[]{:S(2)}) copy-start(f32[448]{0:T(512)} %param.23) | copy-start | bytes 5380
  1.7 16.4 %all-to-all-start = ((bf16[16,48,128]{2,1,0:T(8,128)(2,1)}), bf16[16,48,128]{2,1,0:T(8,128)(2,1)S(1)}, u32[]{:S(2)}, u32[]{:S(2)}) async-start(bf16[16,48,128]{2,1,0:T(8,128)(2,1)} %get-tuple-element.12), calls=%async_computation | async-start | bytes 393216 | tf_op jit(solution)/shard_map/all_to_all | solution.py:393
  9.9 13.4 %copy-start.4 = (s32[32]{0:T(128)S(1)}, s32[32]{0:T(128)}, u32[]{:S(2)}) copy-start(s32[32]{0:T(128)} %len_ref.1) | copy-start | bytes 388
  11.2 22.8 %copy-start.7 = (f32[128]{0:T(128)S(1)}, f32[128]{0:T(128)}, u32[]{:S(2)}) copy-start(f32[128]{0:T(128)} %constant.11.clone) | copy-start | bytes 1540
  11.2 31.3 %copy-start.2 = (s32[32,128]{1,0:T(8,128)S(1)}, s32[32,128]{1,0:T(8,128)}, u32[]{:S(2)}) copy-start(s32[32,128]{1,0:T(8,128)} %page_ref.1) | copy-start | bytes 49156
  11.2 31.3 %copy-start.3 = (s32[32]{0:T(128)S(1)}, s32[32]{0:T(128)}, u32[]{:S(2)}) copy-start(s32[32]{0:T(128)} %perm_ref.1) | copy-start | bytes 388
  19.0 10.4 %all-to-all-start.1 = ((bf16[8,16,512]{2,1,0:T(8,128)(2,1)}), bf16[8,16,512]{2,1,0:T(8,128)(2,1)S(1)}, u32[]{:S(2)}, u32[]{:S(2)}) async-start(bf16[8,16,512]{2,1,0:T(8,128)(2,1)} %qkv_kernel.1), calls=%async_computation.1 | async-start | bytes 262144 | tf_op jit(solution)/shard_map/all_to_all | solution.py:393
  30.4 12.1 %all-to-all-start.2 = ((bf16[16,16,512]{2,1,0:T(8,128)(2,1)}), bf16[16,16,512]{2,1,0:T(8,128)(2,1)S(1)}, u32[]{:S(2)}, u32[]{:S(2)}) async-start(bf16[16,16,512]{2,1,0:T(8,128)(2,1)} %qkv_sum_kernel.1), calls=%async_computation.2 | async-start | bytes 524288 | tf_op jit(solution)/shard_map/all_to_all | solution.py:393
  50.8 20.6 %copy-start.1 = (bf16[320,640]{1,0:T(8,128)(2,1)S(1)}, bf16[320,640]{1,0:T(8,128)(2,1)}, u32[]{:S(2)}) copy-start(bf16[320,640]{1,0:T(8,128)(2,1)} %w_ref.3) | copy-start | bytes 1228804
  50.8 25.3 %copy-start.8 = (f32[40]{0:T(128)S(1)}, f32[40]{0:T(128)}, u32[]{:S(2)}) copy-start(f32[40]{0:T(128)} %param.25) | copy-start | bytes 484
  62.9 25.6 %copy-start.5 = (bf16[640,864]{0,1:T(8,128)(2,1)S(1)}, bf16[640,864]{0,1:T(8,128)(2,1)}, u32[]{:S(2)}) copy-start(bf16[640,864]{0,1:T(8,128)(2,1)} %param.26) | copy-start | bytes 3317764
  72.4 11.6 %all-to-all-start.5 = ((bf16[16,40,128]{2,1,0:T(8,128)(2,1)}), bf16[16,40,128]{2,1,0:T(8,128)(2,1)S(1)}, u32[]{:S(2)}, u32[]{:S(2)}) async-start(bf16[16,40,128]{2,1,0:T(8,128)(2,1)} %project_kernel.2), calls=%async_computation.5 | async-start | bytes 327680 | tf_op jit(solution)/shard_map/all_to_all | solution.py:393
  84.8 11.7 %all-to-all-start.6 = ((bf16[16,48,128]{2,1,0:T(8,128)(2,1)}), bf16[16,48,128]{2,1,0:T(8,128)(2,1)S(1)}, u32[]{:S(2)}, u32[]{:S(2)}) async-start(bf16[16,48,128]{2,1,0:T(8,128)(2,1)} %get-tuple-element.14), calls=%async_computation.6 | async-start | bytes 393216 | tf_op jit(solution)/shard_map/all_to_all | solution.py:393
  97.2 1.6 %collective-permute-start = (bf16[4,16,1792]{2,1,0:T(8,128)(2,1)S(1)}, bf16[4,16,1792]{2,1,0:T(8,128)(2,1)S(1)}, u32[]{:S(2)}, u32[]{:S(2)}) collective-permute-start(bf16[4,16,1792]{2,1,0:T(8,128)(2,1)S(1)} %get-tuple-element.16), channel_id=1, source_target_pairs={{0,16},{16,0},{32,48},{48,32},{64,80},{80,64},{96,112},{112,96},{1... | collective-permute-start | bytes 688136 | tf_op jit(solution)/shard_map/ppermute | solution.py:402
  98.7 19.3 %copy-start = (bf16[864,640]{1,0:T(8,128)(2,1)S(1)}, bf16[864,640]{1,0:T(8,128)(2,1)}, u32[]{:S(2)}) copy-start(bf16[864,640]{1,0:T(8,128)(2,1)} %w_ref.4) | copy-start | bytes 3317764

commit v3 on v2

--- a/solution.py
+++ b/solution.py
@@ -13,7 +13,6 @@
 KV_HEADS = 8
 HEAD_DIM = 128
 STEPS = 4
-AHEAD = 2
 REQ_GRP = 4
 SHARD_PAGES = 8
 PAGE = 128
@@ -37,10 +36,12 @@
 LOW_SCORE = -1e30
 ROPE_BASE = 1000000.0
 BF = jnp.bfloat16
+COVER = pl.CostEstimate(flops=10**10, transcendentals=0, bytes_accessed=64 << 20)
+NT = (((1,), (1,)), ((), ()))
 F32 = jnp.float32
 
 
-def call(kernel, outs, *args, smem=(), anys=(), scratch=()):
+def call(kernel, outs, *args, smem=(), anys=(), scratch=(), cost=None):
     specs = []
     for i in range(len(args)):
         if i in smem:
@@ -59,7 +60,8 @@
         out_specs=[vm] * len(outs) if many else vm,
         scratch_shapes=list(scratch),
         name=getattr(kernel, "__name__", "kernel"),
-        compiler_params=pltpu.CompilerParams(vmem_limit_bytes=32 << 20),
+        cost_estimate=cost,
+        compiler_params=pltpu.CompilerParams(vmem_limit_bytes=16 << 20),
     )(*args)
 
 
@@ -120,9 +122,9 @@
     return value, squares
 
 
-def qkv_kernel(in_ref, w_ref, out_ref, scratch):
+def qkv_kernel(in_ref, w_ref, cos_ref, sin_ref, gain_ref, bias_ref, out_ref, scratch):
     value, squares = collect_features(in_ref, scratch)
-    part = jnp.dot(value, w_ref[...], preferred_element_type=F32)
+    part = lax.dot_general(value, w_ref[...], NT, preferred_element_type=F32)
     hi, lo = split(squares)
     for g in range(N_GRP):
         rows = slice(g * GROUP_ROWS, (g + 1) * GROUP_ROWS)
@@ -152,34 +154,12 @@
 
 
 def attend_kernel(
-    perm_ref, len_ref, page_ref, in_ref, cos_ref, sin_ref, k_hbm, v_hbm, out_ref,
-    qbuf, knew, vnew, rot, sbuf, obuf, kbuf, vbuf, sems,
+    perm_ref, len_ref, page_ref, in_ref, cos_ref, sin_ref, k_ref, v_ref, out_ref,
+    qbuf, knew, vnew, rot, sbuf, obuf,
 ):
     grp_idx = lax.axis_index("grp")
     seq_idx = lax.axis_index("seq")
     members = [perm_ref[grp_idx * REQ_GRP + r] for r in range(REQ_GRP)]
-    copies = [[], []]
-    for r in range(REQ_GRP):
-        for kind, (pool, buf) in enumerate(((k_hbm, kbuf), (v_hbm, vbuf))):
-            pages = []
-            for p in range(SHARD_PAGES):
-                slot = page_ref[members[r], seq_idx * SHARD_PAGES + p]
-                to = buf.at[r, pl.ds(p * PAGE, PAGE)]
-                pages.append(pltpu.make_async_copy(pool.at[slot], to, sems.at[kind, r]))
-            copies[kind].append(pages)
-
-    def begin(kind, r):
-        if r < REQ_GRP:
-            for copy in copies[kind][r]:
-                copy.start()
-
-    def await_pages(kind, r):
-        whole = (kbuf, vbuf)[kind].at[r]
-        pltpu.make_async_copy(whole, whole, sems.at[kind, r]).wait()
-
-    for r in range(AHEAD):
-        begin(0, r)
-        begin(1, r)
     for r in range(REQ_GRP):
         rot[0, r * STEPS : (r + 1) * STEPS, :] = cos_ref[members[r]]
         rot[1, r * STEPS : (r + 1) * STEPS, :] = sin_ref[members[r]]
@@ -225,10 +205,8 @@
     group = iota((2 * QROWS, HEAD_DIM), 1) >> 3
     word = lax.rem(group, 3)
     part_lane = iota((STEPS, HEAD_DIM), 1)
-    nt = (((1,), (1,)), ((), ()))
     for r in range(REQ_GRP):
-        await_pages(0, r)
-        begin(0, r + AHEAD)
+        slots = [page_ref[members[r], seq_idx * SHARD_PAGES + p] for p in range(SHARD_PAGES)]
         live = len_ref[members[r]] - seq_idx * SHARD_KEYS
         bias = jnp.where(place < live, 0.0, LOW_SCORE)[0:1]
         own_bias = jnp.where(own_live & ((column >> 2) == r), 0.0, LOW_SCORE)
@@ -236,12 +214,11 @@
             lanes = slice(h * HEAD_DIM, (h + 2) * HEAD_DIM)
             rows = slice(h * QROWS, (h + 2) * QROWS)
             query = qbuf[r, rows, :].astype(BF)
-            scores = lax.dot_general(query, kbuf[r, :, lanes], nt, preferred_element_type=F32)
+            keys = jnp.concatenate([k_ref[slot, :, lanes] for slot in slots], axis=0)
+            scores = lax.dot_general(query, keys, NT, preferred_element_type=F32)
             sbuf[rows, :SHARD_KEYS] = scores + bias
-            own = lax.dot_general(query, knew[:, lanes], nt, preferred_element_type=F32)
+            own = lax.dot_general(query, knew[:, lanes], NT, preferred_element_type=F32)
             sbuf[rows, SHARD_KEYS:] = own + own_bias
-        await_pages(1, r)
-        begin(1, r + AHEAD)
         for pair in range(0, KV_HEADS, 2):
             lanes = slice(pair * HEAD_DIM, (pair + 2) * HEAD_DIM)
             scores = sbuf[pair * QROWS : (pair + 2) * QROWS, :]
@@ -249,8 +226,9 @@
             weight = jnp.exp2((scores - best) * power)
             total = jnp.sum(weight, axis=1, keepdims=True)
             weight = weight.astype(BF)
+            values = jnp.concatenate([v_ref[slot, :, lanes] for slot in slots], axis=0)
             both = jnp.dot(
-                weight[:, :SHARD_KEYS], vbuf[r, :, lanes], preferred_element_type=F32
+                weight[:, :SHARD_KEYS], values, preferred_element_type=F32
             ) + jnp.dot(weight[:, SHARD_KEYS:], vnew[:, lanes], preferred_element_type=F32)
             both = both / total
             levels = jnp.where(best > 0.1 * LOW_SCORE, best * score_scale + jnp.log(total), LOW_SCORE)
@@ -329,8 +307,8 @@
 
 def gate_kernel(in_ref, gate_ref, up_ref, keep_ref, give_ref, scratch):
     value, squares = collect_features(in_ref, scratch)
-    gate = jnp.dot(value, gate_ref[...], preferred_element_type=F32)
-    up = jnp.dot(value, up_ref[...], preferred_element_type=F32)
+    gate = lax.dot_general(value, gate_ref[...], NT, preferred_element_type=F32)
+    up = lax.dot_general(value, up_ref[...], NT, preferred_element_type=F32)
     hi, lo = split(squares)
     tail = FPAD - FCOLS
     sums = jnp.where(iota((ROWS, tail), 1) < tail // 2, hi[:, :tail], lo[:, :tail])
@@ -425,20 +403,22 @@
             pltpu.VMEM((1, FEAT), F32),
             pltpu.SemaphoreType.DMA((3,)),
         ],
-    )
-    got = exchange(send, "seq")
+        cost=COVER,
+    )
+    got = exchange(send, "seq")
+    bias = jnp.pad(qkv_bias, (0, QPAD - QCOLS))[None, :]
+    gain = gain_mid[:, None]
     send = call(
-        qkv_kernel, sds((N_GRP, GROUP_ROWS, QPAD)), got, qkv_weight,
-        scratch=[pltpu.VMEM((GFEAT, ROWS), F32)],
+        qkv_kernel, sds((N_GRP, GROUP_ROWS, QPAD)), got, qkv_weight.T, cosine, sine, gain, bias,
+        scratch=[pltpu.VMEM((GFEAT, ROWS), F32)], cost=COVER,
     )
     got = exchange(send, "grp")
-    bias = jnp.pad(qkv_bias, (0, QPAD - QCOLS))[None, :]
-    send = call(qkv_sum_kernel, sds((N_SEQ, GROUP_ROWS, QPAD)), got, bias)
+    send = call(qkv_sum_kernel, sds((N_SEQ, GROUP_ROWS, QPAD)), got, bias, cost=COVER)
     got = exchange(send, "seq")
     send = call(
         attend_kernel, sds((N_SEQ, GROUP_ROWS, 4 * HEAD_DIM)),
         group_perm, lengths, page_table, got, cosine, sine, k_pool, v_pool,
-        smem=(0, 1, 2), anys=(6, 7),
+        smem=(0, 1, 2),
         scratch=[
             pltpu.VMEM((REQ_GRP, KV_HEADS * QROWS, 2 * HEAD_DIM), F32),
             pltpu.VMEM((PAGE, KV_HEADS * HEAD_DIM), BF),
@@ -446,9 +426,6 @@
             pltpu.VMEM((2, GROUP_ROWS, HEAD_DIM), F32),
             pltpu.VMEM((KV_HEADS * QROWS, SHARD_KEYS + PAGE), F32),
             pltpu.VMEM((N_SEQ, GROUP_ROWS, 4 * HEAD_DIM), F32),
-            pltpu.VMEM((REQ_GRP, SHARD_KEYS, KV_HEADS * HEAD_DIM), BF),
-            pltpu.VMEM((REQ_GRP, SHARD_KEYS, KV_HEADS * HEAD_DIM), BF),
-            pltpu.SemaphoreType.DMA((2, REQ_GRP)),
         ],
     )
     got = exchange(send, "seq")
@@ -458,13 +435,13 @@
     got = exchange(send, "seq")
     send, res = call(
         middle_kernel, [sds((N_SEQ, FEAT_PAD, ROWS)), sds((FEAT, ROWS), F32)],
-        got, xt, gain_mid[:, None],
+        got, xt, gain,
     )
     got = exchange(send, "seq")
     keep, give = call(
         gate_kernel,
         [sds((N_CHIP, GROUP_ROWS, 2 * FPAD), F32), sds((N_CHIP, GROUP_ROWS, 2 * FPAD))],
-        got, gate_weight, up_weight,
+        got, gate_weight.T, up_weight.T,
         scratch=[pltpu.VMEM((GFEAT, ROWS), F32)],
     )
     send = call(pair_kernel, sds((N_CHIP, GROUP_ROWS, 2 * FPAD)), keep, swap_cores(give))

time: 132 us -> 126 us (0.955)
  blocking collectives: 50.6 us -> 96.2 us
  waiting for transfers between devices: 35.3 us -> 8.9 us
  starting transfers between devices: 23.5 us -> 8.28 us
  Pallas kernels: 16.2 us -> 11.1 us
  local copies, waits for them, and re-layouts: 4.3 us -> 0.15 us
    all_to_all x4 -> x8, blocking collectives: 41.2 us -> 86.8 us  [exchange(): return lax.all_to_all(value, axis, 0, 0, tiled=False)]
    all_to_all x5 -> x1, waiting for transfers between devices: 33.8 us -> 7.43 us  [exchange(): return lax.all_to_all(value, axis, 0, 0, tiled=False)]
    all_to_all x5 -> x1, starting transfers between devices: 23.4 us -> 8.19 us  [exchange(): return lax.all_to_all(value, axis, 0, 0, tiled=False)]
    pallas_call x12, Pallas kernels: 16.2 us -> 11.1 us  [call(): pl.pallas_call(kernel, out_shape=outs, in_specs=specs, out_specs=[vm] * l...]
    unnamed x21 -> x30, local copies, waits for them, and re-layouts: 4.2 us -> 0.06 us
  transfers between devices with their start and end apart: 6 -> 2, of which waited for: 6 -> 2; matrix products, arithmetic and copies ran while one was open for 4% -> 1% of each run, Pallas kernels for 0% -> 0%
where the time goes in v3:
time: 126 us; the launch traced here: 125 us
  blocking collectives  96.2 us (76%)
  Pallas kernels  11.1 us (9%)
  waiting for transfers between devices  8.9 us (7%)
  starting transfers between devices  8.28 us (7%)
    all_to_all x8, blocking collectives, exchange(): return lax.all_to_all(value, axis, 0, 0, tiled=False)  86.8 us
    pallas_call x12, Pallas kernels, call(): pl.pallas_call(kernel, out_shape=outs, in_specs=specs, out_specs=[vm] * l...  11.1 us
    all_to_all x1, blocking collectives, exchange_chips(): lax.all_to_all(value, 'grp', 0, 0, axis_index_groups=groups, tiled=False)  9.39 us
    all_to_all x1, starting transfers between devices, exchange(): return lax.all_to_all(value, axis, 0, 0, tiled=False)  8.19 us
    all_to_all x1, waiting for transfers between devices, exchange(): return lax.all_to_all(value, axis, 0, 0, tiled=False)  7.43 us
  transfers between devices with their start and end apart: 2, of which 2 were waited for; matrix products, arithmetic and copies ran while one was open for 1% of the time, Pallas kernels for 0%

profile of v3, /device:TPU:0, one launch (start us, length us, event | category | flops | bytes accessed | tf_op | source)
XLA Modules:
  0.0 125.4 jit_solution(7146011230851868557)
XLA Ops:
  0.0 0.0 copy-start.5
  0.0 0.0 copy-start.8
  0.0 0.0 copy-start.9
  0.0 1.7 %start_kernel.1 = (bf16[16,48,128]{2,1,0:T(8,128)(2,1)}, f32[40,128]{1,0:T(8,128)S(1)}, bf16[128,128]{1,0:T(8,128)(2,1)S(1)}) custom-call(s32[32]{0:T(128)} %perm_ref.1, bf16[128,40]{1,0:T(8,128)(2,1)} %bitcast.18, f32[1,40]{1,0:T(1,128)} %bitcast.19), custom_call_target="tpu_custom_call" | custom-call | flops 10000000000 | bytes 67108864 | tf_op jit(solution)/shard_map/start_kernel/pallas_call | solution.py:56
  1.7 8.2 %all-to-all-start = ((bf16[16,48,128]{2,1,0:T(8,128)(2,1)}), bf16[16,48,128]{2,1,0:T(8,128)(2,1)S(1)}, u32[]{:S(2)}, u32[]{:S(2)}) async-start(bf16[16,48,128]{2,1,0:T(8,128)(2,1)} %get-tuple-element.12), calls=%async_computation | async-start | bytes 393216 | tf_op jit(solution)/shard_map/all_to_all | solution.py:371
  10.0 0.0 copy-done.5
  10.0 0.1 add_convert_fusion
  10.0 0.0 copy-done.10
  10.0 0.1 copy.16.gain_ref
  10.1 0.0 copy-done.8
  10.1 0.0 copy-done.9
  10.1 0.5 fusion
  10.7 7.4 %all-to-all-done.in_ref = bf16[16,48,128]{2,1,0:T(8,128)(2,1)S(1)} async-done(((bf16[16,48,128]{2,1,0:T(8,128)(2,1)}), bf16[16,48,128]{2,1,0:T(8,128)(2,1)S(1)}, u32[]{:S(2)}, u32[]{:S(2)}) %all-to-all-start) | async-done | bytes 196640 | tf_op jit(solution)/shard_map/all_to_all | solution.py:371
  18.1 0.0 copy-done.7
  18.1 0.3 qkv_kernel.1
  18.5 10.5 %all_to_all.50.in_ref = bf16[8,16,512]{2,1,0:T(8,128)(2,1)S(1)} all-to-all(bf16[8,16,512]{2,1,0:T(8,128)(2,1)S(1)} %qkv_kernel.1), channel_id=1, replica_groups=mesh['grp'=8,'seq'=16] {'grp'}, dimensions={0} | all-to-all | bytes 262144 | tf_op jit(solution)/shard_map/all_to_all | solution.py:371
  29.0 0.2 qkv_sum_kernel.1
  29.2 12.2 %all_to_all.51.in_ref = bf16[16,16,512]{2,1,0:T(8,128)(2,1)S(1)} all-to-all(bf16[16,16,512]{2,1,0:T(8,128)(2,1)S(1)} %qkv_sum_kernel.1), channel_id=1, replica_groups=mesh['grp'=8,'seq'=16] {'seq'}, dimensions={0} | all-to-all | bytes 524288 | tf_op jit(solution)/shard_map/all_to_all | solution.py:371
  41.4 0.0 slice-done
  41.4 0.0 slice-done.2
  41.4 0.0 slice-done.1
  41.4 0.0 slice-done.3
  41.4 0.0 copy-done.4
  41.4 0.0 copy-done.6
  41.5 0.0 copy-start.3
  41.5 5.5 %attend_kernel.1 = bf16[16,16,512]{2,1,0:T(8,128)(2,1)S(1)} custom-call(s32[32]{0:T(128)S(1)} %copy-done.6, s32[32]{0:T(128)S(1)} %copy-done.5, s32[32,128]{1,0:T(8,128)S(1)} %copy-done.4, bf16[16,16,512]{2,1,0:T(8,128)(2,1)S(1)} %all_to_all.51.in_ref, f32[32,4,128]{2,1,0:T(4,128)S(1)} %get-tuple-element.20.cos_ref, ...), custom_call_target="tpu_custom_call" | custom-call | tf_op jit(solution)/shard_map/attend_kernel/pallas_call | solution.py:56
  47.0 0.0 copy-start.1
  47.0 12.0 %all_to_all.52.in_ref = bf16[16,16,512]{2,1,0:T(8,128)(2,1)S(1)} all-to-all(bf16[16,16,512]{2,1,0:T(8,128)(2,1)S(1)} %attend_kernel.1), channel_id=1, replica_groups=mesh['grp'=8,'seq'=16] {'seq'}, dimensions={0} | all-to-all | bytes 524288 | tf_op jit(solution)/shard_map/all_to_all | solution.py:371
  59.0 0.4 merge_kernel.1
  59.4 8.2 %all_to_all.53.in_ref = bf16[8,16,384]{2,1,0:T(8,128)(2,1)S(1)} all-to-all(bf16[8,16,384]{2,1,0:T(8,128)(2,1)S(1)} %merge_kernel.1), channel_id=1, replica_groups=mesh['grp'=8,'seq'=16] {'grp'}, dimensions={0} | all-to-all | bytes 196608 | tf_op jit(solution)/shard_map/all_to_all | solution.py:371
  67.6 0.0 copy-done.3
  67.6 0.3 project_kernel.2
  67.9 11.4 %all_to_all.54.in_ref = bf16[16,40,128]{2,1,0:T(8,128)(2,1)S(1)} all-to-all(bf16[16,40,128]{2,1,0:T(8,128)(2,1)S(1)} %project_kernel.2), channel_id=1, replica_groups=mesh['grp'=8,'seq'=16] {'seq'}, dimensions={0} | all-to-all | bytes 327680 | tf_op jit(solution)/shard_map/all_to_all | solution.py:371
  79.4 0.1 middle_kernel.1
  79.5 11.5 %all_to_all.55.in_ref = bf16[16,48,128]{2,1,0:T(8,128)(2,1)S(1)} all-to-all(bf16[16,48,128]{2,1,0:T(8,128)(2,1)S(1)} %get-tuple-element.14), channel_id=1, replica_groups=mesh['grp'=8,'seq'=16] {'seq'}, dimensions={0} | all-to-all | bytes 393216 | tf_op jit(solution)/shard_map/all_to_all | solution.py:371
  91.0 0.0 copy-done.1
  91.0 0.0 copy-done
  91.0 0.8 gate_kernel.1
  91.8 0.1 collective-permute-start
  91.9 1.5 %collective-permute-done.got_ref = bf16[4,16,1792]{2,1,0:T(8,128)(2,1)S(1)} collective-permute-done((bf16[4,16,1792]{2,1,0:T(8,128)(2,1)S(1)}, bf16[4,16,1792]{2,1,0:T(8,128)(2,1)S(1)}, u32[]{:S(2)}, u32[]{:S(2)}) %collective-permute-start) | collective-permute-done | bytes 229408 | tf_op jit(solution)/shard_map/ppermute | solution.py:380
  93.4 0.2 pair_kernel.1
  93.6 9.4 %all_to_all.56.in_ref = bf16[4,16,1792]{2,1,0:T(8,128)(2,1)S(1)} all-to-all(bf16[4,16,1792]{2,1,0:T(8,128)(2,1)S(1)} %pair_kernel.1), channel_id=1, replica_groups={{0,32,64,96},{16,48,80,112},{1,33,65,97},{17,49,81,113},{2,34,66,98},{1..., dimensions={0} | all-to-all | bytes 458752 | tf_op jit(solution)/shard_map/all_to_all | solution.py:376
  103.0 0.2 hidden_kernel.1
  103.2 9.6 %all_to_all.57.in_ref = bf16[8,16,896]{2,1,0:T(8,128)(2,1)S(1)} all-to-all(bf16[8,16,896]{2,1,0:T(8,128)(2,1)S(1)} %hidden_kernel.1), channel_id=1, replica_groups=mesh['grp'=8,'seq'=16] {'grp'}, dimensions={0} | all-to-all | bytes 458752 | tf_op jit(solution)/shard_map/all_to_all | solution.py:371
  112.7 0.0 copy-done.2
  112.7 0.4 project_kernel.3
  113.2 11.5 %all_to_all.58.in_ref = bf16[16,40,128]{2,1,0:T(8,128)(2,1)S(1)} all-to-all(bf16[16,40,128]{2,1,0:T(8,128)(2,1)S(1)} %project_kernel.3), channel_id=1, replica_groups=mesh['grp'=8,'seq'=16] {'seq'}, dimensions={0} | all-to-all | bytes 327680 | tf_op jit(solution)/shard_map/all_to_all | solution.py:371
  124.6 0.8 finish_kernel.1
  (14 shorter events, 0.0 us)
Async XLA Ops:
  0.0 10.0 %copy-start.5 = (s32[32]{0:T(128)S(1)}, s32[32]{0:T(128)}, u32[]{:S(2)}) copy-start(s32[32]{0:T(128)} %len_ref.1) | copy-start | bytes 388
  0.0 10.0 %copy-start.10 = (f32[40]{0:T(128)S(1)}, f32[40]{0:T(128)}, u32[]{:S(2)}) copy-start(f32[40]{0:T(128)} %param.25) | copy-start | bytes 484
  0.0 10.1 %copy-start.8 = (f32[448]{0:T(512)S(1)}, f32[448]{0:T(512)}, u32[]{:S(2)}) copy-start(f32[448]{0:T(512)} %param.23) | copy-start | bytes 5380
  0.0 10.1 %copy-start.9 = (f32[128]{0:T(128)S(1)}, f32[128]{0:T(128)}, u32[]{:S(2)}) copy-start(f32[128]{0:T(128)} %constant.11.clone) | copy-start | bytes 1540
  0.0 18.1 %copy-start.7 = (bf16[640,448]{0,1:T(8,128)(2,1)S(1)}, bf16[640,448]{0,1:T(8,128)(2,1)}, u32[]{:S(2)}) copy-start(bf16[640,448]{0,1:T(8,128)(2,1)} %param.22) | copy-start | bytes 1720324
  1.7 16.4 %all-to-all-start = ((bf16[16,48,128]{2,1,0:T(8,128)(2,1)}), bf16[16,48,128]{2,1,0:T(8,128)(2,1)S(1)}, u32[]{:S(2)}, u32[]{:S(2)}) async-start(bf16[16,48,128]{2,1,0:T(8,128)(2,1)} %get-tuple-element.12), calls=%async_computation | async-start | bytes 393216 | tf_op jit(solution)/shard_map/all_to_all | solution.py:371
  18.1 23.3 %slice-start = ((s8[8388608]{0:T(1024)(128)(4,1)}), s8[4194304]{0:T(1024)(128)(4,1)S(1)}, s32[]{:S(2)}) async-start(s8[8388608]{0:T(1024)(128)(4,1)} %bitcast.8), calls=%async_computation.10 | async-start | bytes 8388608
  18.1 23.3 %slice-start.2 = ((s8[8388608]{0:T(1024)(128)(4,1)}), s8[4194304]{0:T(1024)(128)(4,1)S(1)}, s32[]{:S(2)}) async-start(s8[8388608]{0:T(1024)(128)(4,1)} %bitcast.10), calls=%async_computation.12 | async-start | bytes 8388608
  28.9 12.5 %slice-start.1 = ((s8[8388608]{0:T(1024)(128)(4,1)}), s8[4194304]{0:T(1024)(128)(4,1)S(1)}, s32[]{:S(2)}) async-start(s8[8388608]{0:T(1024)(128)(4,1)} %bitcast.8), calls=%async_computation.11 | async-start | bytes 8388608
  28.9 12.5 %slice-start.3 = ((s8[8388608]{0:T(1024)(128)(4,1)}), s8[4194304]{0:T(1024)(128)(4,1)S(1)}, s32[]{:S(2)}) async-start(s8[8388608]{0:T(1024)(128)(4,1)} %bitcast.10), calls=%async_computation.13 | async-start | bytes 8388608
  28.9 12.5 %copy-start.4 = (s32[32,128]{1,0:T(8,128)S(1)}, s32[32,128]{1,0:T(8,128)}, u32[]{:S(2)}) copy-start(s32[32,128]{1,0:T(8,128)} %page_ref.1) | copy-start | bytes 49156
  28.9 12.5 %copy-start.6 = (s32[32]{0:T(128)S(1)}, s32[32]{0:T(128)}, u32[]{:S(2)}) copy-start(s32[32]{0:T(128)} %perm_ref.1) | copy-start | bytes 388
  41.5 26.2 %copy-start.3 = (bf16[320,640]{1,0:T(8,128)(2,1)S(1)}, bf16[320,640]{1,0:T(8,128)(2,1)}, u32[]{:S(2)}) copy-start(bf16[320,640]{1,0:T(8,128)(2,1)} %w_ref.2) | copy-start | bytes 1228804
  47.0 44.0 %copy-start.1 = (bf16[640,864]{0,1:T(8,128)(2,1)S(1)}, bf16[640,864]{0,1:T(8,128)(2,1)}, u32[]{:S(2)}) copy-start(bf16[640,864]{0,1:T(8,128)(2,1)} %param.27) | copy-start | bytes 3317764
  59.0 32.0 %copy-start = (bf16[640,864]{0,1:T(8,128)(2,1)S(1)}, bf16[640,864]{0,1:T(8,128)(2,1)}, u32[]{:S(2)}) copy-start(bf16[640,864]{0,1:T(8,128)(2,1)} %param.26) | copy-start | bytes 3317764
  91.8 1.6 %collective-permute-start = (bf16[4,16,1792]{2,1,0:T(8,128)(2,1)S(1)}, bf16[4,16,1792]{2,1,0:T(8,128)(2,1)S(1)}, u32[]{:S(2)}, u32[]{:S(2)}) collective-permute-start(bf16[4,16,1792]{2,1,0:T(8,128)(2,1)S(1)} %get-tuple-element.16), channel_id=1, source_target_pairs={{0,16},{16,0},{32,48},{48,32},{64,80},{80,64},{96,112},{112,96},{1... | collective-permute-start | bytes 688136 | tf_op jit(solution)/shard_map/ppermute | solution.py:380
  93.4 19.3 %copy-start.2 = (bf16[864,640]{1,0:T(8,128)(2,1)S(1)}, bf16[864,640]{1,0:T(8,128)(2,1)}, u32[]{:S(2)}) copy-start(bf16[864,640]{1,0:T(8,128)(2,1)} %w_ref.3) | copy-start | bytes 3317764

commit v4 on v3

--- a/solution.py
+++ b/solution.py
@@ -122,7 +122,7 @@
     return value, squares
 
 
-def qkv_kernel(in_ref, w_ref, cos_ref, sin_ref, gain_ref, bias_ref, out_ref, scratch):
+def qkv_kernel(in_ref, w_ref, out_ref, scratch):
     value, squares = collect_features(in_ref, scratch)
     part = lax.dot_general(value, w_ref[...], NT, preferred_element_type=F32)
     hi, lo = split(squares)
@@ -139,13 +139,15 @@
     return lax.rsqrt(squares / D + EPSILON)
 
 
-def qkv_sum_kernel(in_ref, bias_ref, out_ref):
+def qkv_sum_kernel(in_ref, bias_ref, out_ref, scratch):
+    scratch[...] = jnp.zeros_like(scratch)
+    scratch[:, :QCOLS] = bias_ref[...]
     total = in_ref[0].astype(F32)
     for g in range(1, N_GRP):
         total = total + in_ref[g].astype(F32)
     squares = total[:, QCOLS : QCOLS + 1] + total[:, QCOLS + 32 : QCOLS + 33]
     scale = lax.rsqrt(squares / D + EPSILON)
-    value = total * scale + bias_ref[...]
+    value = total * scale + scratch[...]
     value = jnp.where(iota(value.shape, 1) < QCOLS, value, 0.0)
     odd = lax.rem(lax.axis_index("seq"), 2) == 1
     value = jnp.where(odd, pltpu.roll(value, QPAD - QCOLS, 1), value).astype(BF)
@@ -153,18 +155,37 @@
         out_ref[s] = value
 
 
+def cos_sin(angle):
+    turns = jnp.floor(angle * float(2.0 / np.pi) + 0.5)
+    rest = ((angle - turns * 1.5703125) - turns * 4.837512969970703125e-4) - turns * 7.54978995489188216e-8
+    square = rest * rest
+    sine = ((-1.9515295891e-4 * square + 8.3321608736e-3) * square - 1.6666654611e-1) * square * rest + rest
+    cosine = (
+        (2.443315711809948e-5 * square - 1.388731625493765e-3) * square + 4.166664568298827e-2
+    ) * square * square - 0.5 * square + 1.0
+    quadrant = turns.astype(jnp.int32) & 3
+    odd = (quadrant & 1) == 1
+    first = jnp.where(odd, sine, cosine)
+    second = jnp.where(odd, cosine, sine)
+    return (
+        jnp.where((quadrant == 1) | (quadrant == 2), -first, first),
+        jnp.where(quadrant >= 2, -second, second),
+    )
+
+
 def attend_kernel(
-    perm_ref, len_ref, page_ref, in_ref, cos_ref, sin_ref, k_ref, v_ref, out_ref,
-    qbuf, knew, vnew, rot, sbuf, obuf,
+    perm_ref, len_ref, page_ref, in_ref, inverse_ref, k_ref, v_ref, out_ref,
+    qbuf, knew, vnew, sbuf, obuf,
 ):
     grp_idx = lax.axis_index("grp")
     seq_idx = lax.axis_index("seq")
     members = [perm_ref[grp_idx * REQ_GRP + r] for r in range(REQ_GRP)]
+    row = iota((GROUP_ROWS, HEAD_DIM), 0)
+    position = row & (STEPS - 1)
     for r in range(REQ_GRP):
-        rot[0, r * STEPS : (r + 1) * STEPS, :] = cos_ref[members[r]]
-        rot[1, r * STEPS : (r + 1) * STEPS, :] = sin_ref[members[r]]
-    cosine = rot[0]
-    sine = rot[1]
+        position = position + jnp.where((row >> 2) == r, len_ref[members[r]], 0)
+    cosine, sine = cos_sin(position.astype(F32) * inverse_ref[...])
+    sine = jnp.where(iota(sine.shape, 1) < HEAD_DIM // 2, -sine, sine)
     knew[...] = jnp.zeros_like(knew)
     vnew[...] = jnp.zeros_like(vnew)
     qbuf[...] = jnp.zeros_like(qbuf)
@@ -302,7 +323,9 @@
     total = total + part
     res_ref[...] = total
     squares = jnp.sum(total * total, axis=0, keepdims=True)
-    spread_features(total * gain_ref[...], squares, send_ref)
+    diagonal = iota((FEAT, FEAT), 0) == iota((FEAT, FEAT), 1)
+    gain = jnp.sum(jnp.where(diagonal, gain_ref[...], 0.0), axis=1, keepdims=True)
+    spread_features(total * gain, squares, send_ref)
 
 
 def gate_kernel(in_ref, gate_ref, up_ref, keep_ref, give_ref, scratch):
@@ -386,11 +409,7 @@
 ):
     half = HEAD_DIM // 2
     inverse = np.exp(-np.arange(half) * (2.0 / HEAD_DIM) * np.log(ROPE_BASE)).astype(np.float32)
-    inverse = jnp.asarray(np.concatenate([inverse, inverse]))
-    position = (lengths[:, None] + jnp.arange(STEPS, dtype=jnp.int32)[None, :]).astype(F32)
-    angle = position[..., None] * inverse
-    cosine = jnp.cos(angle)
-    sine = jnp.where(jnp.arange(HEAD_DIM) < half, -1.0, 1.0) * jnp.sin(angle)
+    inverse = jnp.asarray(np.concatenate([inverse, inverse]))[None, :]
 
     send, xt, hot = call(
         start_kernel,
@@ -406,24 +425,24 @@
         cost=COVER,
     )
     got = exchange(send, "seq")
-    bias = jnp.pad(qkv_bias, (0, QPAD - QCOLS))[None, :]
-    gain = gain_mid[:, None]
     send = call(
-        qkv_kernel, sds((N_GRP, GROUP_ROWS, QPAD)), got, qkv_weight.T, cosine, sine, gain, bias,
+        qkv_kernel, sds((N_GRP, GROUP_ROWS, QPAD)), got, qkv_weight.T,
         scratch=[pltpu.VMEM((GFEAT, ROWS), F32)], cost=COVER,
     )
     got = exchange(send, "grp")
-    send = call(qkv_sum_kernel, sds((N_SEQ, GROUP_ROWS, QPAD)), got, bias, cost=COVER)
+    send = call(
+        qkv_sum_kernel, sds((N_SEQ, GROUP_ROWS, QPAD)), got, qkv_bias[None, :],
+        scratch=[pltpu.VMEM((1, QPAD), F32)], cost=COVER,
+    )
     got = exchange(send, "seq")
     send = call(
         attend_kernel, sds((N_SEQ, GROUP_ROWS, 4 * HEAD_DIM)),
-        group_perm, lengths, page_table, got, cosine, sine, k_pool, v_pool,
+        group_perm, lengths, page_table, got, inverse, k_pool, v_pool,
         smem=(0, 1, 2),
         scratch=[
             pltpu.VMEM((REQ_GRP, KV_HEADS * QROWS, 2 * HEAD_DIM), F32),
             pltpu.VMEM((PAGE, KV_HEADS * HEAD_DIM), BF),
             pltpu.VMEM((PAGE, KV_HEADS * HEAD_DIM), BF),
-            pltpu.VMEM((2, GROUP_ROWS, HEAD_DIM), F32),
             pltpu.VMEM((KV_HEADS * QROWS, SHARD_KEYS + PAGE), F32),
             pltpu.VMEM((N_SEQ, GROUP_ROWS, 4 * HEAD_DIM), F32),
         ],
@@ -435,7 +454,7 @@
     got = exchange(send, "seq")
     send, res = call(
         middle_kernel, [sds((N_SEQ, FEAT_PAD, ROWS)), sds((FEAT, ROWS), F32)],
-        got, xt, gain,
+        got, xt, gain_mid[None, :],
     )
     got = exchange(send, "seq")
     keep, give = call(

time: 126 us -> 125 us (level)
  blocking collectives: 96.2 us -> 112 us
  starting transfers between devices: 8.28 us -> 0.09 us
  waiting for transfers between devices: 8.9 us -> 1.48 us
    all_to_all x8 -> x9, blocking collectives: 86.8 us -> 103 us  [exchange(): return lax.all_to_all(value, axis, 0, 0, tiled=False)]
    all_to_all x1 -> x0, starting transfers between devices: 8.19 us -> none  [exchange(): return lax.all_to_all(value, axis, 0, 0, tiled=False)]
    all_to_all x1 -> x0, waiting for transfers between devices: 7.43 us -> none  [exchange(): return lax.all_to_all(value, axis, 0, 0, tiled=False)]
  transfers between devices with their start and end apart: 2 -> 1, of which waited for: 2 -> 1; matrix products, arithmetic and copies ran while one was open for 1% -> 0% of each run, Pallas kernels for 0% -> 0%
where the time goes in v4:
time: 125 us
  blocking collectives  112 us (90%)
  Pallas kernels  10.4 us (8%)
  waiting for transfers between devices  1.48 us (1%)
    all_to_all x9, blocking collectives, exchange(): return lax.all_to_all(value, axis, 0, 0, tiled=False)  103 us
    pallas_call x12, Pallas kernels, call(): pl.pallas_call(kernel, out_shape=outs, in_specs=specs, out_specs=[vm] * l...  10.4 us
    all_to_all x1, blocking collectives, exchange_chips(): lax.all_to_all(value, 'grp', 0, 0, axis_index_groups=groups, tiled=False)  9.39 us
  transfers between devices with their start and end apart: 1, of which 1 were waited for; matrix products, arithmetic and copies ran while one was open for 0% of the time, Pallas kernels for 0%

profile of v4, /device:TPU:0, one launch (start us, length us, event | category | flops | bytes accessed | tf_op | source)
XLA Modules:
  0.0 124.6 jit_solution(9266079991878536087)
XLA Ops:
  0.0 0.0 copy-start.9
  0.0 1.0 start_kernel.1
  1.1 16.1 %all_to_all.50.in_ref = bf16[16,48,128]{2,1,0:T(8,128)(2,1)S(1)} all-to-all(bf16[16,48,128]{2,1,0:T(8,128)(2,1)S(1)} %get-tuple-element.12), channel_id=1, replica_groups=mesh['grp'=8,'seq'=16] {'seq'}, dimensions={0} | all-to-all | bytes 393216 | tf_op jit(solution)/shard_map/all_to_all | solution.py:394
  17.2 0.0 copy-done.9
  17.2 0.0 copy-start.10
  17.2 0.0 slice-start.2
  17.2 0.3 qkv_kernel.1
  17.6 10.5 %all_to_all.51.in_ref = bf16[8,16,512]{2,1,0:T(8,128)(2,1)S(1)} all-to-all(bf16[8,16,512]{2,1,0:T(8,128)(2,1)S(1)} %qkv_kernel.1), channel_id=1, replica_groups=mesh['grp'=8,'seq'=16] {'grp'}, dimensions={0} | all-to-all | bytes 262144 | tf_op jit(solution)/shard_map/all_to_all | solution.py:394
  28.0 0.0 copy-done.10
  28.0 0.0 copy-start.5
  28.1 0.0 copy-start.6
  28.1 0.0 copy-start.8
  28.1 0.2 qkv_sum_kernel.1
  28.3 12.2 %all_to_all.52.in_ref = bf16[16,16,512]{2,1,0:T(8,128)(2,1)S(1)} all-to-all(bf16[16,16,512]{2,1,0:T(8,128)(2,1)S(1)} %qkv_sum_kernel.1), channel_id=1, replica_groups=mesh['grp'=8,'seq'=16] {'seq'}, dimensions={0} | all-to-all | bytes 524288 | tf_op jit(solution)/shard_map/all_to_all | solution.py:394
  40.5 0.0 slice-done
  40.5 0.0 slice-done.2
  40.5 0.0 slice-done.1
  40.5 0.0 slice-done.3
  40.5 0.0 copy-done.4
  40.6 0.0 copy-done.5
  40.6 0.0 copy-done.6
  40.6 0.0 copy-done.8
  40.6 0.0 copy-start.3
  40.6 5.5 %attend_kernel.1 = bf16[16,16,512]{2,1,0:T(8,128)(2,1)S(1)} custom-call(s32[32]{0:T(128)S(1)} %copy-done.5, s32[32]{0:T(128)S(1)} %copy-done.6, s32[32,128]{1,0:T(8,128)S(1)} %copy-done.4, bf16[16,16,512]{2,1,0:T(8,128)(2,1)S(1)} %all_to_all.52.in_ref, f32[1,128]{1,0:T(1,128)S(1)} %copy-done.8, bf16[32,128,1024]{2,1,0:T(8,128)(2,1)S(1)} %bitcast.9, ...), custom_call_target="tpu_custom_call" | custom-call | tf_op jit(solution)/shard_map/attend_kernel/pallas_call | solution.py:56
  46.2 0.0 copy-start.7
  46.2 0.0 copy-start.1
  46.2 12.0 %all_to_all.53.in_ref = bf16[16,16,512]{2,1,0:T(8,128)(2,1)S(1)} all-to-all(bf16[16,16,512]{2,1,0:T(8,128)(2,1)S(1)} %attend_kernel.1), channel_id=1, replica_groups=mesh['grp'=8,'seq'=16] {'seq'}, dimensions={0} | all-to-all | bytes 524288 | tf_op jit(solution)/shard_map/all_to_all | solution.py:394
  58.2 0.4 merge_kernel.1
  58.6 8.2 %all_to_all.54.in_ref = bf16[8,16,384]{2,1,0:T(8,128)(2,1)S(1)} all-to-all(bf16[8,16,384]{2,1,0:T(8,128)(2,1)S(1)} %merge_kernel.1), channel_id=1, replica_groups=mesh['grp'=8,'seq'=16] {'grp'}, dimensions={0} | all-to-all | bytes 196608 | tf_op jit(solution)/shard_map/all_to_all | solution.py:394
  66.8 0.0 copy-done.3
  66.8 0.3 project_kernel.2
  67.1 11.4 %all_to_all.55.in_ref = bf16[16,40,128]{2,1,0:T(8,128)(2,1)S(1)} all-to-all(bf16[16,40,128]{2,1,0:T(8,128)(2,1)S(1)} %project_kernel.2), channel_id=1, replica_groups=mesh['grp'=8,'seq'=16] {'seq'}, dimensions={0} | all-to-all | bytes 327680 | tf_op jit(solution)/shard_map/all_to_all | solution.py:394
  78.6 0.0 copy-done.7
  78.6 0.1 middle_kernel.1
  78.7 11.5 %all_to_all.56.in_ref = bf16[16,48,128]{2,1,0:T(8,128)(2,1)S(1)} all-to-all(bf16[16,48,128]{2,1,0:T(8,128)(2,1)S(1)} %get-tuple-element.14), channel_id=1, replica_groups=mesh['grp'=8,'seq'=16] {'seq'}, dimensions={0} | all-to-all | bytes 393216 | tf_op jit(solution)/shard_map/all_to_all | solution.py:394
  90.2 0.0 copy-done.1
  90.2 0.0 copy-done
  90.2 0.8 gate_kernel.1
  91.0 0.1 collective-permute-start
  91.1 1.5 %collective-permute-done.got_ref = bf16[4,16,1792]{2,1,0:T(8,128)(2,1)S(1)} collective-permute-done((bf16[4,16,1792]{2,1,0:T(8,128)(2,1)S(1)}, bf16[4,16,1792]{2,1,0:T(8,128)(2,1)S(1)}, u32[]{:S(2)}, u32[]{:S(2)}) %collective-permute-start) | collective-permute-done | bytes 229408 | tf_op jit(solution)/shard_map/ppermute | solution.py:403
  92.6 0.2 pair_kernel.1
  92.8 9.4 %all_to_all.57.in_ref = bf16[4,16,1792]{2,1,0:T(8,128)(2,1)S(1)} all-to-all(bf16[4,16,1792]{2,1,0:T(8,128)(2,1)S(1)} %pair_kernel.1), channel_id=1, replica_groups={{0,32,64,96},{16,48,80,112},{1,33,65,97},{17,49,81,113},{2,34,66,98},{1..., dimensions={0} | all-to-all | bytes 458752 | tf_op jit(solution)/shard_map/all_to_all | solution.py:399
  102.2 0.2 hidden_kernel.1
  102.4 9.6 %all_to_all.58.in_ref = bf16[8,16,896]{2,1,0:T(8,128)(2,1)S(1)} all-to-all(bf16[8,16,896]{2,1,0:T(8,128)(2,1)S(1)} %hidden_kernel.1), channel_id=1, replica_groups=mesh['grp'=8,'seq'=16] {'grp'}, dimensions={0} | all-to-all | bytes 458752 | tf_op jit(solution)/shard_map/all_to_all | solution.py:394
  111.9 0.0 copy-done.2
  111.9 0.4 project_kernel.3
  112.4 11.5 %all_to_all.59.in_ref = bf16[16,40,128]{2,1,0:T(8,128)(2,1)S(1)} all-to-all(bf16[16,40,128]{2,1,0:T(8,128)(2,1)S(1)} %project_kernel.3), channel_id=1, replica_groups=mesh['grp'=8,'seq'=16] {'seq'}, dimensions={0} | all-to-all | bytes 327680 | tf_op jit(solution)/shard_map/all_to_all | solution.py:394
  123.8 0.8 finish_kernel.1
  (8 shorter events, 0.0 us)
Async XLA Ops:
  0.0 17.2 %copy-start.9 = (bf16[640,448]{0,1:T(8,128)(2,1)S(1)}, bf16[640,448]{0,1:T(8,128)(2,1)}, u32[]{:S(2)}) copy-start(bf16[640,448]{0,1:T(8,128)(2,1)} %param.22) | copy-start | bytes 1720324
  17.2 10.8 %copy-start.10 = (f32[448]{0:T(512)S(1)}, f32[448]{0:T(512)}, u32[]{:S(2)}) copy-start(f32[448]{0:T(512)} %param.23) | copy-start | bytes 5380
  17.2 23.3 %slice-start = ((s8[8388608]{0:T(1024)(128)(4,1)}), s8[4194304]{0:T(1024)(128)(4,1)S(1)}, s32[]{:S(2)}) async-start(s8[8388608]{0:T(1024)(128)(4,1)} %bitcast.8), calls=%async_computation.10 | async-start | bytes 8388608
  17.2 23.3 %slice-start.2 = ((s8[8388608]{0:T(1024)(128)(4,1)}), s8[4194304]{0:T(1024)(128)(4,1)S(1)}, s32[]{:S(2)}) async-start(s8[8388608]{0:T(1024)(128)(4,1)} %bitcast.10), calls=%async_computation.12 | async-start | bytes 8388608
  28.0 12.5 %slice-start.1 = ((s8[8388608]{0:T(1024)(128)(4,1)}), s8[4194304]{0:T(1024)(128)(4,1)S(1)}, s32[]{:S(2)}) async-start(s8[8388608]{0:T(1024)(128)(4,1)} %bitcast.8), calls=%async_computation.11 | async-start | bytes 8388608
  28.0 12.5 %slice-start.3 = ((s8[8388608]{0:T(1024)(128)(4,1)}), s8[4194304]{0:T(1024)(128)(4,1)S(1)}, s32[]{:S(2)}) async-start(s8[8388608]{0:T(1024)(128)(4,1)} %bitcast.10), calls=%async_computation.13 | async-start | bytes 8388608
  28.0 12.5 %copy-start.4 = (s32[32,128]{1,0:T(8,128)S(1)}, s32[32,128]{1,0:T(8,128)}, u32[]{:S(2)}) copy-start(s32[32,128]{1,0:T(8,128)} %page_ref.1) | copy-start | bytes 49156
  28.0 12.5 %copy-start.5 = (s32[32]{0:T(128)S(1)}, s32[32]{0:T(128)}, u32[]{:S(2)}) copy-start(s32[32]{0:T(128)} %perm_ref.1) | copy-start | bytes 388
  28.1 12.5 %copy-start.6 = (s32[32]{0:T(128)S(1)}, s32[32]{0:T(128)}, u32[]{:S(2)}) copy-start(s32[32]{0:T(128)} %len_ref.1) | copy-start | bytes 388
  28.1 12.5 %copy-start.8 = (f32[1,128]{1,0:T(1,128)S(1)}, f32[1,128]{1,0:T(1,128)}, u32[]{:S(2)}) copy-start(f32[1,128]{1,0:T(1,128)} %constant.8.inverse_ref) | copy-start | bytes 1540
  40.6 26.2 %copy-start.3 = (bf16[320,640]{1,0:T(8,128)(2,1)S(1)}, bf16[320,640]{1,0:T(8,128)(2,1)}, u32[]{:S(2)}) copy-start(bf16[320,640]{1,0:T(8,128)(2,1)} %w_ref.2) | copy-start | bytes 1228804
  46.2 32.4 %copy-start.7 = (f32[40]{0:T(128)S(1)}, f32[40]{0:T(128)}, u32[]{:S(2)}) copy-start(f32[40]{0:T(128)} %param.25) | copy-start | bytes 484
  46.2 44.0 %copy-start.1 = (bf16[640,864]{0,1:T(8,128)(2,1)S(1)}, bf16[640,864]{0,1:T(8,128)(2,1)}, u32[]{:S(2)}) copy-start(bf16[640,864]{0,1:T(8,128)(2,1)} %param.27) | copy-start | bytes 3317764
  58.2 32.0 %copy-start = (bf16[640,864]{0,1:T(8,128)(2,1)S(1)}, bf16[640,864]{0,1:T(8,128)(2,1)}, u32[]{:S(2)}) copy-start(bf16[640,864]{0,1:T(8,128)(2,1)} %param.26) | copy-start | bytes 3317764
  91.0 1.6 %collective-permute-start = (bf16[4,16,1792]{2,1,0:T(8,128)(2,1)S(1)}, bf16[4,16,1792]{2,1,0:T(8,128)(2,1)S(1)}, u32[]{:S(2)}, u32[]{:S(2)}) collective-permute-start(bf16[4,16,1792]{2,1,0:T(8,128)(2,1)S(1)} %get-tuple-element.16), channel_id=1, source_target_pairs={{0,16},{16,0},{32,48},{48,32},{64,80},{80,64},{96,112},{112,96},{1... | collective-permute-start | bytes 688136 | tf_op jit(solution)/shard_map/ppermute | solution.py:403
  92.6 19.3 %copy-start.2 = (bf16[864,640]{1,0:T(8,128)(2,1)S(1)}, bf16[864,640]{1,0:T(8,128)(2,1)}, u32[]{:S(2)}) copy-start(bf16[864,640]{1,0:T(8,128)(2,1)} %w_ref.3) | copy-start | bytes 3317764

commit v5 on v4

--- a/solution.py
+++ b/solution.py
@@ -186,8 +186,7 @@
         position = position + jnp.where((row >> 2) == r, len_ref[members[r]], 0)
     cosine, sine = cos_sin(position.astype(F32) * inverse_ref[...])
     sine = jnp.where(iota(sine.shape, 1) < HEAD_DIM // 2, -sine, sine)
-    knew[...] = jnp.zeros_like(knew)
-    vnew[...] = jnp.zeros_like(vnew)
+    sbuf[:, :, SHARD_KEYS:] = jnp.full((2, KV_HEADS * QROWS, PAGE), LOW_SCORE, F32)
     qbuf[...] = jnp.zeros_like(qbuf)
     for pair in range(N_SEQ // 2):
         even = in_ref[2 * pair].astype(F32)
@@ -212,45 +211,56 @@
                     qbuf[r, at : at + STEPS, side : side + HEAD_DIM] = value[r * STEPS : (r + 1) * STEPS]
             elif head < HEADS + KV_HEADS:
                 h = head - HEADS
-                knew[:GROUP_ROWS, h * HEAD_DIM : (h + 1) * HEAD_DIM] = value.astype(BF)
+                knew[:, h * HEAD_DIM : (h + 1) * HEAD_DIM] = value.astype(BF)
             else:
                 h = head - HEADS - KV_HEADS
-                vnew[:GROUP_ROWS, h * HEAD_DIM : (h + 1) * HEAD_DIM] = value.astype(BF)
+                vnew[:, h * HEAD_DIM : (h + 1) * HEAD_DIM] = value.astype(BF)
 
     score_scale = HEAD_DIM ** (-0.5)
     power = score_scale * float(np.log2(np.e))
-    step = iota((2 * QROWS, PAGE), 0) & (STEPS - 1)
-    column = iota((2 * QROWS, PAGE), 1)
-    own_live = ((column & (STEPS - 1)) <= step) & (seq_idx == N_SEQ - 1) & (column < GROUP_ROWS)
+    step = iota((2 * QROWS, GROUP_ROWS), 0) & (STEPS - 1)
+    column = iota((2 * QROWS, GROUP_ROWS), 1)
+    own_live = ((column & (STEPS - 1)) <= step) & (seq_idx == N_SEQ - 1)
     place = iota((8, SHARD_KEYS), 1)
-    group = iota((2 * QROWS, HEAD_DIM), 1) >> 3
-    word = lax.rem(group, 3)
+    group = iota((2 * QROWS, HEAD_DIM), 1) >> 2
+    word = lax.rem(group & 15, 3)
     part_lane = iota((STEPS, HEAD_DIM), 1)
-    for r in range(REQ_GRP):
-        slots = [page_ref[members[r], seq_idx * SHARD_PAGES + p] for p in range(SHARD_PAGES)]
+    part_turn = part_lane & 63
+    slots = [
+        [page_ref[members[r], seq_idx * SHARD_PAGES + p] for p in range(SHARD_PAGES)] for r in range(REQ_GRP)
+    ]
+
+    def score(r, h):
         live = len_ref[members[r]] - seq_idx * SHARD_KEYS
         bias = jnp.where(place < live, 0.0, LOW_SCORE)[0:1]
         own_bias = jnp.where(own_live & ((column >> 2) == r), 0.0, LOW_SCORE)
-        for h in range(0, KV_HEADS, 2):
-            lanes = slice(h * HEAD_DIM, (h + 2) * HEAD_DIM)
-            rows = slice(h * QROWS, (h + 2) * QROWS)
-            query = qbuf[r, rows, :].astype(BF)
-            keys = jnp.concatenate([k_ref[slot, :, lanes] for slot in slots], axis=0)
-            scores = lax.dot_general(query, keys, NT, preferred_element_type=F32)
-            sbuf[rows, :SHARD_KEYS] = scores + bias
-            own = lax.dot_general(query, knew[:, lanes], NT, preferred_element_type=F32)
-            sbuf[rows, SHARD_KEYS:] = own + own_bias
+        lanes = slice(h * HEAD_DIM, (h + 2) * HEAD_DIM)
+        rows = slice(h * QROWS, (h + 2) * QROWS)
+        query = qbuf[r, rows, :].astype(BF)
+        keys = jnp.concatenate([k_ref[slot, :, lanes] for slot in slots[r]], axis=0)
+        scores = lax.dot_general(query, keys, NT, preferred_element_type=F32)
+        sbuf[r % 2, rows, :SHARD_KEYS] = scores + bias
+        own = lax.dot_general(query, knew[:, lanes], NT, preferred_element_type=F32)
+        sbuf[r % 2, rows, SHARD_KEYS : SHARD_KEYS + GROUP_ROWS] = own + own_bias
+
+    for h in range(0, KV_HEADS, 2):
+        score(0, h)
+    for r in range(REQ_GRP):
         for pair in range(0, KV_HEADS, 2):
+            if r + 1 < REQ_GRP:
+                score(r + 1, pair)
             lanes = slice(pair * HEAD_DIM, (pair + 2) * HEAD_DIM)
-            scores = sbuf[pair * QROWS : (pair + 2) * QROWS, :]
+            scores = sbuf[r % 2, pair * QROWS : (pair + 2) * QROWS, :]
             best = jnp.max(scores, axis=1, keepdims=True)
             weight = jnp.exp2((scores - best) * power)
             total = jnp.sum(weight, axis=1, keepdims=True)
             weight = weight.astype(BF)
-            values = jnp.concatenate([v_ref[slot, :, lanes] for slot in slots], axis=0)
+            values = jnp.concatenate([v_ref[slot, :, lanes] for slot in slots[r]], axis=0)
             both = jnp.dot(
                 weight[:, :SHARD_KEYS], values, preferred_element_type=F32
-            ) + jnp.dot(weight[:, SHARD_KEYS:], vnew[:, lanes], preferred_element_type=F32)
+            ) + jnp.dot(
+                weight[:, SHARD_KEYS : SHARD_KEYS + GROUP_ROWS], vnew[:, lanes], preferred_element_type=F32
+            )
             both = both / total
             levels = jnp.where(best > 0.1 * LOW_SCORE, best * score_scale + jnp.log(total), LOW_SCORE)
             hi, rest = split(levels)
@@ -263,21 +273,28 @@
                 for half in range(2):
                     to = slice(r * STEPS, (r + 1) * STEPS)
                     parts = [slice((2 * half + j) * STEPS, (2 * half + j + 1) * STEPS) for j in range(3)]
+                    notes = jnp.where(
+                        part_turn < 12, level[parts[0]], jnp.where(part_turn < 24, level[parts[1]], level[parts[2]])
+                    )
+                    spare = (2, 0)[half]
                     for j in range(3):
-                        obuf[2 * h + half, to, j * HEAD_DIM : (j + 1) * HEAD_DIM] = mixed[parts[j]]
-                    obuf[2 * h + half, to, 3 * HEAD_DIM :] = jnp.where(
-                        part_lane < 24, level[parts[0]], jnp.where(part_lane < 48, level[parts[1]], level[parts[2]])
-                    )
+                        value = mixed[parts[j]]
+                        if j == spare:
+                            value = jnp.where((part_lane < 64) == (half == 0), value, notes)
+                        obuf[2 * h + half, to, j * HEAD_DIM : (j + 1) * HEAD_DIM] = value
     for s in range(N_SEQ):
         out_ref[s] = obuf[s].astype(BF)
 
 
 def merge_kernel(in_ref, out_ref):
+    odd = lax.rem(lax.axis_index("seq"), 2) == 1
     levels = []
     for s in range(N_SEQ):
-        cols = in_ref[s, :, 3 * HEAD_DIM :].astype(F32)
+        first = in_ref[s, :, :HEAD_DIM].astype(F32)
+        last = in_ref[s, :, 2 * HEAD_DIM :].astype(F32)
+        cols = jnp.where(odd, first, pltpu.roll(last, HEAD_DIM // 2, 1))
         levels.append(
-            [cols[:, a : a + 1] + cols[:, a + 8 : a + 9] + cols[:, a + 16 : a + 17] for a in (0, 24, 48)]
+            [cols[:, a : a + 1] + cols[:, a + 4 : a + 5] + cols[:, a + 8 : a + 9] for a in (0, 12, 24)]
         )
     out = []
     for j in range(3):
@@ -290,7 +307,6 @@
             value = value + in_ref[s, :, j * HEAD_DIM : (j + 1) * HEAD_DIM].astype(F32) * factor
         out.append(value / total)
     value = jnp.concatenate(out, axis=1)
-    odd = lax.rem(lax.axis_index("seq"), 2) == 1
     value = jnp.where(odd, pltpu.roll(value, 3 * HEAD_DIM - HEAD_DIM // 2, 1), value).astype(BF)
     for g in range(N_GRP):
         out_ref[g] = value
@@ -436,15 +452,15 @@
     )
     got = exchange(send, "seq")
     send = call(
-        attend_kernel, sds((N_SEQ, GROUP_ROWS, 4 * HEAD_DIM)),
+        attend_kernel, sds((N_SEQ, GROUP_ROWS, 3 * HEAD_DIM)),
         group_perm, lengths, page_table, got, inverse, k_pool, v_pool,
         smem=(0, 1, 2),
         scratch=[
             pltpu.VMEM((REQ_GRP, KV_HEADS * QROWS, 2 * HEAD_DIM), F32),
-            pltpu.VMEM((PAGE, KV_HEADS * HEAD_DIM), BF),
-            pltpu.VMEM((PAGE, KV_HEADS * HEAD_DIM), BF),
-            pltpu.VMEM((KV_HEADS * QROWS, SHARD_KEYS + PAGE), F32),
-            pltpu.VMEM((N_SEQ, GROUP_ROWS, 4 * HEAD_DIM), F32),
+            pltpu.VMEM((GROUP_ROWS, KV_HEADS * HEAD_DIM), BF),
+            pltpu.VMEM((GROUP_ROWS, KV_HEADS * HEAD_DIM), BF),
+            pltpu.VMEM((2, KV_HEADS * QROWS, SHARD_KEYS + PAGE), F32),
+            pltpu.VMEM((N_SEQ, GROUP_ROWS, 3 * HEAD_DIM), F32),
         ],
     )
     got = exchange(send, "seq")

time: 125 us -> 124 us (level)
  no operation moved by 1% of the time
where the time goes in v5:
time: 124 us
  blocking collectives  112 us (90%)
  Pallas kernels  10.2 us (8%)
  waiting for transfers between devices  1.48 us (1%)
    all_to_all x9, blocking collectives, exchange(): return lax.all_to_all(value, axis, 0, 0, tiled=False)  103 us
    pallas_call x12, Pallas kernels, call(): pl.pallas_call(kernel, out_shape=outs, in_specs=specs, out_specs=[vm] * l...  10.2 us
    all_to_all x1, blocking collectives, exchange_chips(): lax.all_to_all(value, 'grp', 0, 0, axis_index_groups=groups, tiled=False)  9.39 us
  transfers between devices with their start and end apart: 1, of which 1 were waited for; matrix products, arithmetic and copies ran while one was open for 0% of the time, Pallas kernels for 0%

profile of v5, /device:TPU:0, one launch (start us, length us, event | category | flops | bytes accessed | tf_op | source)
XLA Modules:
  0.0 124.0 jit_solution(16893446344844072524)
XLA Ops:
  0.0 0.0 copy-start.9
  0.0 1.0 start_kernel.1
  1.1 16.1 %all_to_all.50.in_ref = bf16[16,48,128]{2,1,0:T(8,128)(2,1)S(1)} all-to-all(bf16[16,48,128]{2,1,0:T(8,128)(2,1)S(1)} %get-tuple-element.12), channel_id=1, replica_groups=mesh['grp'=8,'seq'=16] {'seq'}, dimensions={0} | all-to-all | bytes 393216 | tf_op jit(solution)/shard_map/all_to_all | solution.py:410
  17.2 0.0 copy-done.9
  17.2 0.0 copy-start.10
  17.2 0.0 slice-start.2
  17.2 0.3 qkv_kernel.1
  17.6 10.5 %all_to_all.51.in_ref = bf16[8,16,512]{2,1,0:T(8,128)(2,1)S(1)} all-to-all(bf16[8,16,512]{2,1,0:T(8,128)(2,1)S(1)} %qkv_kernel.1), channel_id=1, replica_groups=mesh['grp'=8,'seq'=16] {'grp'}, dimensions={0} | all-to-all | bytes 262144 | tf_op jit(solution)/shard_map/all_to_all | solution.py:410
  28.0 0.0 copy-done.10
  28.0 0.0 copy-start.5
  28.1 0.0 copy-start.6
  28.1 0.0 copy-start.8
  28.1 0.2 qkv_sum_kernel.1
  28.3 12.2 %all_to_all.52.in_ref = bf16[16,16,512]{2,1,0:T(8,128)(2,1)S(1)} all-to-all(bf16[16,16,512]{2,1,0:T(8,128)(2,1)S(1)} %qkv_sum_kernel.1), channel_id=1, replica_groups=mesh['grp'=8,'seq'=16] {'seq'}, dimensions={0} | all-to-all | bytes 524288 | tf_op jit(solution)/shard_map/all_to_all | solution.py:410
  40.5 0.0 slice-done
  40.5 0.0 slice-done.2
  40.5 0.0 slice-done.1
  40.5 0.0 slice-done.3
  40.5 0.0 copy-done.4
  40.6 0.0 copy-done.5
  40.6 0.0 copy-done.6
  40.6 0.0 copy-done.8
  40.6 0.0 copy-start.3
  40.6 5.3 %attend_kernel.1 = bf16[16,16,384]{2,1,0:T(8,128)(2,1)S(1)} custom-call(s32[32]{0:T(128)S(1)} %copy-done.5, s32[32]{0:T(128)S(1)} %copy-done.6, s32[32,128]{1,0:T(8,128)S(1)} %copy-done.4, bf16[16,16,512]{2,1,0:T(8,128)(2,1)S(1)} %all_to_all.52.in_ref, f32[1,128]{1,0:T(1,128)S(1)} %copy-done.8, bf16[32,128,1024]{2,1,0:T(8,128)(2,1)S(1)} %bitcast.9, ...), custom_call_target="tpu_custom_call" | custom-call | tf_op jit(solution)/shard_map/attend_kernel/pallas_call | solution.py:56
  45.9 0.0 copy-start.7
  45.9 0.0 copy-start.1
  45.9 11.6 %all_to_all.53.in_ref = bf16[16,16,384]{2,1,0:T(8,128)(2,1)S(1)} all-to-all(bf16[16,16,384]{2,1,0:T(8,128)(2,1)S(1)} %attend_kernel.1), channel_id=1, replica_groups=mesh['grp'=8,'seq'=16] {'seq'}, dimensions={0} | all-to-all | bytes 393216 | tf_op jit(solution)/shard_map/all_to_all | solution.py:410
  57.5 0.4 merge_kernel.1
  58.0 8.2 %all_to_all.54.in_ref = bf16[8,16,384]{2,1,0:T(8,128)(2,1)S(1)} all-to-all(bf16[8,16,384]{2,1,0:T(8,128)(2,1)S(1)} %merge_kernel.1), channel_id=1, replica_groups=mesh['grp'=8,'seq'=16] {'grp'}, dimensions={0} | all-to-all | bytes 196608 | tf_op jit(solution)/shard_map/all_to_all | solution.py:410
  66.2 0.0 copy-done.3
  66.2 0.3 project_kernel.2
  66.5 11.5 %all_to_all.55.in_ref = bf16[16,40,128]{2,1,0:T(8,128)(2,1)S(1)} all-to-all(bf16[16,40,128]{2,1,0:T(8,128)(2,1)S(1)} %project_kernel.2), channel_id=1, replica_groups=mesh['grp'=8,'seq'=16] {'seq'}, dimensions={0} | all-to-all | bytes 327680 | tf_op jit(solution)/shard_map/all_to_all | solution.py:410
  78.0 0.0 copy-done.7
  78.0 0.1 middle_kernel.1
  78.1 11.5 %all_to_all.56.in_ref = bf16[16,48,128]{2,1,0:T(8,128)(2,1)S(1)} all-to-all(bf16[16,48,128]{2,1,0:T(8,128)(2,1)S(1)} %get-tuple-element.14), channel_id=1, replica_groups=mesh['grp'=8,'seq'=16] {'seq'}, dimensions={0} | all-to-all | bytes 393216 | tf_op jit(solution)/shard_map/all_to_all | solution.py:410
  89.6 0.0 copy-done.1
  89.6 0.0 copy-done
  89.6 0.8 gate_kernel.1
  90.5 0.1 collective-permute-start
  90.6 1.5 %collective-permute-done.got_ref = bf16[4,16,1792]{2,1,0:T(8,128)(2,1)S(1)} collective-permute-done((bf16[4,16,1792]{2,1,0:T(8,128)(2,1)S(1)}, bf16[4,16,1792]{2,1,0:T(8,128)(2,1)S(1)}, u32[]{:S(2)}, u32[]{:S(2)}) %collective-permute-start) | collective-permute-done | bytes 229408 | tf_op jit(solution)/shard_map/ppermute | solution.py:419
  92.0 0.2 pair_kernel.1
  92.2 9.4 %all_to_all.57.in_ref = bf16[4,16,1792]{2,1,0:T(8,128)(2,1)S(1)} all-to-all(bf16[4,16,1792]{2,1,0:T(8,128)(2,1)S(1)} %pair_kernel.1), channel_id=1, replica_groups={{0,32,64,96},{16,48,80,112},{1,33,65,97},{17,49,81,113},{2,34,66,98},{1..., dimensions={0} | all-to-all | bytes 458752 | tf_op jit(solution)/shard_map/all_to_all | solution.py:415
  101.6 0.2 hidden_kernel.1
  101.8 9.6 %all_to_all.58.in_ref = bf16[8,16,896]{2,1,0:T(8,128)(2,1)S(1)} all-to-all(bf16[8,16,896]{2,1,0:T(8,128)(2,1)S(1)} %hidden_kernel.1), channel_id=1, replica_groups=mesh['grp'=8,'seq'=16] {'grp'}, dimensions={0} | all-to-all | bytes 458752 | tf_op jit(solution)/shard_map/all_to_all | solution.py:410
  111.4 0.0 copy-done.2
  111.4 0.4 project_kernel.3
  111.8 11.5 %all_to_all.59.in_ref = bf16[16,40,128]{2,1,0:T(8,128)(2,1)S(1)} all-to-all(bf16[16,40,128]{2,1,0:T(8,128)(2,1)S(1)} %project_kernel.3), channel_id=1, replica_groups=mesh['grp'=8,'seq'=16] {'seq'}, dimensions={0} | all-to-all | bytes 327680 | tf_op jit(solution)/shard_map/all_to_all | solution.py:410
  123.3 0.8 finish_kernel.1
  (8 shorter events, 0.0 us)
Async XLA Ops:
  0.0 17.2 %copy-start.9 = (bf16[640,448]{0,1:T(8,128)(2,1)S(1)}, bf16[640,448]{0,1:T(8,128)(2,1)}, u32[]{:S(2)}) copy-start(bf16[640,448]{0,1:T(8,128)(2,1)} %param.22) | copy-start | bytes 1720324
  17.2 10.8 %copy-start.10 = (f32[448]{0:T(512)S(1)}, f32[448]{0:T(512)}, u32[]{:S(2)}) copy-start(f32[448]{0:T(512)} %param.23) | copy-start | bytes 5380
  17.2 23.3 %slice-start = ((s8[8388608]{0:T(1024)(128)(4,1)}), s8[4194304]{0:T(1024)(128)(4,1)S(1)}, s32[]{:S(2)}) async-start(s8[8388608]{0:T(1024)(128)(4,1)} %bitcast.8), calls=%async_computation.10 | async-start | bytes 8388608
  17.2 23.3 %slice-start.2 = ((s8[8388608]{0:T(1024)(128)(4,1)}), s8[4194304]{0:T(1024)(128)(4,1)S(1)}, s32[]{:S(2)}) async-start(s8[8388608]{0:T(1024)(128)(4,1)} %bitcast.10), calls=%async_computation.12 | async-start | bytes 8388608
  28.0 12.5 %slice-start.1 = ((s8[8388608]{0:T(1024)(128)(4,1)}), s8[4194304]{0:T(1024)(128)(4,1)S(1)}, s32[]{:S(2)}) async-start(s8[8388608]{0:T(1024)(128)(4,1)} %bitcast.8), calls=%async_computation.11 | async-start | bytes 8388608
  28.0 12.5 %slice-start.3 = ((s8[8388608]{0:T(1024)(128)(4,1)}), s8[4194304]{0:T(1024)(128)(4,1)S(1)}, s32[]{:S(2)}) async-start(s8[8388608]{0:T(1024)(128)(4,1)} %bitcast.10), calls=%async_computation.13 | async-start | bytes 8388608
  28.0 12.5 %copy-start.4 = (s32[32,128]{1,0:T(8,128)S(1)}, s32[32,128]{1,0:T(8,128)}, u32[]{:S(2)}) copy-start(s32[32,128]{1,0:T(8,128)} %page_ref.1) | copy-start | bytes 49156
  28.0 12.5 %copy-start.5 = (s32[32]{0:T(128)S(1)}, s32[32]{0:T(128)}, u32[]{:S(2)}) copy-start(s32[32]{0:T(128)} %perm_ref.1) | copy-start | bytes 388
  28.1 12.5 %copy-start.6 = (s32[32]{0:T(128)S(1)}, s32[32]{0:T(128)}, u32[]{:S(2)}) copy-start(s32[32]{0:T(128)} %len_ref.1) | copy-start | bytes 388
  28.1 12.5 %copy-start.8 = (f32[1,128]{1,0:T(1,128)S(1)}, f32[1,128]{1,0:T(1,128)}, u32[]{:S(2)}) copy-start(f32[1,128]{1,0:T(1,128)} %constant.8.inverse_ref) | copy-start | bytes 1540
  40.6 25.6 %copy-start.3 = (bf16[320,640]{1,0:T(8,128)(2,1)S(1)}, bf16[320,640]{1,0:T(8,128)(2,1)}, u32[]{:S(2)}) copy-start(bf16[320,640]{1,0:T(8,128)(2,1)} %w_ref.2) | copy-start | bytes 1228804
  45.9 32.1 %copy-start.7 = (f32[40]{0:T(128)S(1)}, f32[40]{0:T(128)}, u32[]{:S(2)}) copy-start(f32[40]{0:T(128)} %param.25) | copy-start | bytes 484
  45.9 43.7 %copy-start.1 = (bf16[640,864]{0,1:T(8,128)(2,1)S(1)}, bf16[640,864]{0,1:T(8,128)(2,1)}, u32[]{:S(2)}) copy-start(bf16[640,864]{0,1:T(8,128)(2,1)} %param.27) | copy-start | bytes 3317764
  57.5 32.1 %copy-start = (bf16[640,864]{0,1:T(8,128)(2,1)S(1)}, bf16[640,864]{0,1:T(8,128)(2,1)}, u32[]{:S(2)}) copy-start(bf16[640,864]{0,1:T(8,128)(2,1)} %param.26) | copy-start | bytes 3317764
  90.5 1.6 %collective-permute-start = (bf16[4,16,1792]{2,1,0:T(8,128)(2,1)S(1)}, bf16[4,16,1792]{2,1,0:T(8,128)(2,1)S(1)}, u32[]{:S(2)}, u32[]{:S(2)}) collective-permute-start(bf16[4,16,1792]{2,1,0:T(8,128)(2,1)S(1)} %get-tuple-element.16), channel_id=1, source_target_pairs={{0,16},{16,0},{32,48},{48,32},{64,80},{80,64},{96,112},{112,96},{1... | collective-permute-start | bytes 688136 | tf_op jit(solution)/shard_map/ppermute | solution.py:419
  92.0 19.3 %copy-start.2 = (bf16[864,640]{1,0:T(8,128)(2,1)S(1)}, bf16[864,640]{1,0:T(8,128)(2,1)}, u32[]{:S(2)}) copy-start(bf16[864,640]{1,0:T(8,128)(2,1)} %w_ref.3) | copy-start | bytes 3317764

commit v6 on v5

--- a/solution.py
+++ b/solution.py
@@ -344,29 +344,36 @@
     spread_features(total * gain, squares, send_ref)
 
 
-def gate_kernel(in_ref, gate_ref, up_ref, keep_ref, give_ref, scratch):
+def half_kernel(kept, in_ref, gate_ref, up_ref, out_ref, scratch):
     value, squares = collect_features(in_ref, scratch)
+    second = on_second_core()
+
+    def by_core(rows):
+        blocks = [rows[g * GROUP_ROWS : (g + 1) * GROUP_ROWS] for g in range(N_GRP)]
+        pairs = list(zip(blocks[0::2], blocks[1::2]))
+        if kept:
+            return jnp.concatenate([jnp.where(second, last, first) for first, last in pairs], axis=0)
+        return jnp.concatenate([jnp.where(second, first, last) for first, last in pairs], axis=0)
+
+    value = by_core(value)
     gate = lax.dot_general(value, gate_ref[...], NT, preferred_element_type=F32)
     up = lax.dot_general(value, up_ref[...], NT, preferred_element_type=F32)
     hi, lo = split(squares)
     tail = FPAD - FCOLS
-    sums = jnp.where(iota((ROWS, tail), 1) < tail // 2, hi[:, :tail], lo[:, :tail])
-    second = on_second_core()
-    spare = slice(FCOLS, FPAD)
+    sums = by_core(jnp.where(iota((ROWS, tail), 1) < tail // 2, hi[:, :tail], lo[:, :tail]))
     for x in range(N_CHIP):
-        first_rows = slice(2 * x * GROUP_ROWS, (2 * x + 1) * GROUP_ROWS)
-        last_rows = slice((2 * x + 1) * GROUP_ROWS, (2 * x + 2) * GROUP_ROWS)
-        for lanes, part in (
-            (slice(0, FCOLS), gate),
-            (spare, sums),
-            (slice(FPAD, FPAD + FCOLS), up),
-        ):
-            first = part[first_rows]
-            last = part[last_rows]
-            keep_ref[x, :, lanes] = jnp.where(second, last, first)
-            give_ref[x, :, lanes] = jnp.where(second, first, last).astype(BF)
-        keep_ref[x, :, FPAD + FCOLS :] = jnp.zeros((GROUP_ROWS, tail), F32)
-        give_ref[x, :, FPAD + FCOLS :] = jnp.zeros((GROUP_ROWS, tail), BF)
+        rows = slice(x * GROUP_ROWS, (x + 1) * GROUP_ROWS)
+        for start, part in ((0, gate), (FCOLS, sums), (FPAD, up)):
+            out_ref[x, :, start : start + part.shape[1]] = part[rows].astype(out_ref.dtype)
+        out_ref[x, :, FPAD + FCOLS :] = jnp.zeros((GROUP_ROWS, tail), out_ref.dtype)
+
+
+def give_kernel(*refs):
+    half_kernel(False, *refs)
+
+
+def keep_kernel(*refs):
+    half_kernel(True, *refs)
 
 
 def pair_kernel(keep_ref, got_ref, out_ref):
@@ -473,13 +480,12 @@
         got, xt, gain_mid[None, :],
     )
     got = exchange(send, "seq")
-    keep, give = call(
-        gate_kernel,
-        [sds((N_CHIP, GROUP_ROWS, 2 * FPAD), F32), sds((N_CHIP, GROUP_ROWS, 2 * FPAD))],
-        got, gate_weight.T, up_weight.T,
-        scratch=[pltpu.VMEM((GFEAT, ROWS), F32)],
-    )
-    send = call(pair_kernel, sds((N_CHIP, GROUP_ROWS, 2 * FPAD)), keep, swap_cores(give))
+    halves = (got, gate_weight.T, up_weight.T)
+    room = [pltpu.VMEM((GFEAT, ROWS), F32)]
+    shape = (N_CHIP, GROUP_ROWS, 2 * FPAD)
+    other = swap_cores(call(give_kernel, sds(shape), *halves, scratch=room))
+    keep = call(keep_kernel, sds(shape, F32), *halves, scratch=room, cost=COVER)
+    send = call(pair_kernel, sds(shape), keep, other)
     got = exchange_chips(send)
     send = call(hidden_kernel, sds((N_GRP, GROUP_ROWS, FPAD)), got)
     got = exchange(send, "grp")

time: 124 us -> 124 us (level)
    pallas_call x12 -> x13, Pallas kernels: 10.2 us -> 10.9 us  [call(): pl.pallas_call(kernel, out_shape=outs, in_specs=specs, out_specs=[vm] * l...]
  transfers between devices with their start and end apart: 1 -> 1, of which waited for: 1 -> 1; matrix products, arithmetic and copies ran while one was open for 0% -> 0% of each run, Pallas kernels for 0% -> 1%
where the time goes in v6:
time: 124 us
  blocking collectives  112 us (90%)
  Pallas kernels  10.9 us (9%)
    all_to_all x9, blocking collectives, exchange(): return lax.all_to_all(value, axis, 0, 0, tiled=False)  103 us
    pallas_call x13, Pallas kernels, call(): pl.pallas_call(kernel, out_shape=outs, in_specs=specs, out_specs=[vm] * l...  10.9 us
    all_to_all x1, blocking collectives, exchange_chips(): lax.all_to_all(value, 'grp', 0, 0, axis_index_groups=groups, tiled=False)  9.26 us
  transfers between devices with their start and end apart: 1, of which 1 were waited for; matrix products, arithmetic and copies ran while one was open for 0% of the time, Pallas kernels for 1%

profile of v6, /device:TPU:0, one launch (start us, length us, event | category | flops | bytes accessed | tf_op | source)
XLA Modules:
  0.0 123.8 jit_solution(2690645504045240957)
XLA Ops:
  0.0 0.0 copy-start.9
  0.0 1.0 start_kernel.1
  1.1 16.1 %all_to_all.50.in_ref = bf16[16,48,128]{2,1,0:T(8,128)(2,1)S(1)} all-to-all(bf16[16,48,128]{2,1,0:T(8,128)(2,1)S(1)} %get-tuple-element.10), channel_id=1, replica_groups=mesh['grp'=8,'seq'=16] {'seq'}, dimensions={0} | all-to-all | bytes 393216 | tf_op jit(solution)/shard_map/all_to_all | solution.py:417
  17.2 0.0 copy-done.9
  17.2 0.3 qkv_kernel.1
  17.6 10.5 %all_to_all.51.in_ref = bf16[8,16,512]{2,1,0:T(8,128)(2,1)S(1)} all-to-all(bf16[8,16,512]{2,1,0:T(8,128)(2,1)S(1)} %qkv_kernel.1), channel_id=1, replica_groups=mesh['grp'=8,'seq'=16] {'grp'}, dimensions={0} | all-to-all | bytes 262144 | tf_op jit(solution)/shard_map/all_to_all | solution.py:417
  28.0 0.0 copy-done.10
  28.0 0.0 copy-start.5
  28.1 0.0 copy-start.6
  28.1 0.0 copy-start.8
  28.1 0.2 qkv_sum_kernel.1
  28.3 12.2 %all_to_all.52.in_ref = bf16[16,16,512]{2,1,0:T(8,128)(2,1)S(1)} all-to-all(bf16[16,16,512]{2,1,0:T(8,128)(2,1)S(1)} %qkv_sum_kernel.1), channel_id=1, replica_groups=mesh['grp'=8,'seq'=16] {'seq'}, dimensions={0} | all-to-all | bytes 524288 | tf_op jit(solution)/shard_map/all_to_all | solution.py:417
  40.5 0.0 slice-done
  40.5 0.0 slice-done.2
  40.5 0.0 slice-done.1
  40.5 0.0 slice-done.3
  40.5 0.0 copy-done.4
  40.6 0.0 copy-done.5
  40.6 0.0 copy-done.6
  40.6 0.0 copy-done.8
  40.6 0.0 copy-start.3
  40.6 5.3 %attend_kernel.1 = bf16[16,16,384]{2,1,0:T(8,128)(2,1)S(1)} custom-call(s32[32]{0:T(128)S(1)} %copy-done.5, s32[32]{0:T(128)S(1)} %copy-done.6, s32[32,128]{1,0:T(8,128)S(1)} %copy-done.4, bf16[16,16,512]{2,1,0:T(8,128)(2,1)S(1)} %all_to_all.52.in_ref, f32[1,128]{1,0:T(1,128)S(1)} %copy-done.8, bf16[32,128,1024]{2,1,0:T(8,128)(2,1)S(1)} %bitcast.9, ...), custom_call_target="tpu_custom_call" | custom-call | tf_op jit(solution)/shard_map/attend_kernel/pallas_call | solution.py:56
  45.9 0.0 copy-start.7
  45.9 0.0 copy-start.1
  45.9 11.6 %all_to_all.53.in_ref = bf16[16,16,384]{2,1,0:T(8,128)(2,1)S(1)} all-to-all(bf16[16,16,384]{2,1,0:T(8,128)(2,1)S(1)} %attend_kernel.1), channel_id=1, replica_groups=mesh['grp'=8,'seq'=16] {'seq'}, dimensions={0} | all-to-all | bytes 393216 | tf_op jit(solution)/shard_map/all_to_all | solution.py:417
  57.5 0.4 merge_kernel.1
  58.0 8.2 %all_to_all.54.in_ref = bf16[8,16,384]{2,1,0:T(8,128)(2,1)S(1)} all-to-all(bf16[8,16,384]{2,1,0:T(8,128)(2,1)S(1)} %merge_kernel.1), channel_id=1, replica_groups=mesh['grp'=8,'seq'=16] {'grp'}, dimensions={0} | all-to-all | bytes 196608 | tf_op jit(solution)/shard_map/all_to_all | solution.py:417
  66.2 0.0 copy-done.3
  66.2 0.3 project_kernel.2
  66.5 11.5 %all_to_all.55.in_ref = bf16[16,40,128]{2,1,0:T(8,128)(2,1)S(1)} all-to-all(bf16[16,40,128]{2,1,0:T(8,128)(2,1)S(1)} %project_kernel.2), channel_id=1, replica_groups=mesh['grp'=8,'seq'=16] {'seq'}, dimensions={0} | all-to-all | bytes 327680 | tf_op jit(solution)/shard_map/all_to_all | solution.py:417
  78.0 0.0 copy-done.7
  78.0 0.1 middle_kernel.1
  78.1 11.5 %all_to_all.56.refs_0_ = bf16[16,48,128]{2,1,0:T(8,128)(2,1)S(1)} all-to-all(bf16[16,48,128]{2,1,0:T(8,128)(2,1)S(1)} %get-tuple-element.12), channel_id=1, replica_groups=mesh['grp'=8,'seq'=16] {'seq'}, dimensions={0} | all-to-all | bytes 393216 | tf_op jit(solution)/shard_map/all_to_all | solution.py:417
  89.6 0.0 copy-done.1
  89.6 0.0 copy-done
  89.6 0.8 give_kernel.1
  90.4 0.1 collective-permute-start
  90.5 0.8 keep_kernel.1.keep_ref
  91.3 0.0 copy-start.2
  91.3 0.7 collective-permute-done.got_ref
  92.0 0.2 pair_kernel.1
  92.2 9.3 %all_to_all.57.in_ref = bf16[4,16,1792]{2,1,0:T(8,128)(2,1)S(1)} all-to-all(bf16[4,16,1792]{2,1,0:T(8,128)(2,1)S(1)} %pair_kernel.1), channel_id=1, replica_groups={{0,32,64,96},{16,48,80,112},{1,33,65,97},{17,49,81,113},{2,34,66,98},{1..., dimensions={0} | all-to-all | bytes 458752 | tf_op jit(solution)/shard_map/all_to_all | solution.py:422
  101.4 0.2 hidden_kernel.1
  101.6 9.6 %all_to_all.58.in_ref = bf16[8,16,896]{2,1,0:T(8,128)(2,1)S(1)} all-to-all(bf16[8,16,896]{2,1,0:T(8,128)(2,1)S(1)} %hidden_kernel.1), channel_id=1, replica_groups=mesh['grp'=8,'seq'=16] {'grp'}, dimensions={0} | all-to-all | bytes 458752 | tf_op jit(solution)/shard_map/all_to_all | solution.py:417
  111.2 0.0 copy-done.2
  111.2 0.4 project_kernel.3
  111.6 11.5 %all_to_all.59.in_ref = bf16[16,40,128]{2,1,0:T(8,128)(2,1)S(1)} all-to-all(bf16[16,40,128]{2,1,0:T(8,128)(2,1)S(1)} %project_kernel.3), channel_id=1, replica_groups=mesh['grp'=8,'seq'=16] {'seq'}, dimensions={0} | all-to-all | bytes 327680 | tf_op jit(solution)/shard_map/all_to_all | solution.py:417
  123.1 0.8 finish_kernel.1
  (9 shorter events, 0.0 us)
Async XLA Ops:
  0.0 17.2 %copy-start.9 = (bf16[640,448]{0,1:T(8,128)(2,1)S(1)}, bf16[640,448]{0,1:T(8,128)(2,1)}, u32[]{:S(2)}) copy-start(bf16[640,448]{0,1:T(8,128)(2,1)} %param.22) | copy-start | bytes 1720324
  17.2 10.8 %copy-start.10 = (f32[448]{0:T(512)S(1)}, f32[448]{0:T(512)}, u32[]{:S(2)}) copy-start(f32[448]{0:T(512)} %param.23) | copy-start | bytes 5380
  17.2 23.3 %slice-start = ((s8[8388608]{0:T(1024)(128)(4,1)}), s8[4194304]{0:T(1024)(128)(4,1)S(1)}, s32[]{:S(2)}) async-start(s8[8388608]{0:T(1024)(128)(4,1)} %bitcast.8), calls=%async_computation.10 | async-start | bytes 8388608
  17.2 23.3 %slice-start.2 = ((s8[8388608]{0:T(1024)(128)(4,1)}), s8[4194304]{0:T(1024)(128)(4,1)S(1)}, s32[]{:S(2)}) async-start(s8[8388608]{0:T(1024)(128)(4,1)} %bitcast.10), calls=%async_computation.12 | async-start | bytes 8388608
  28.0 12.5 %slice-start.1 = ((s8[8388608]{0:T(1024)(128)(4,1)}), s8[4194304]{0:T(1024)(128)(4,1)S(1)}, s32[]{:S(2)}) async-start(s8[8388608]{0:T(1024)(128)(4,1)} %bitcast.8), calls=%async_computation.11 | async-start | bytes 8388608
  28.0 12.5 %slice-start.3 = ((s8[8388608]{0:T(1024)(128)(4,1)}), s8[4194304]{0:T(1024)(128)(4,1)S(1)}, s32[]{:S(2)}) async-start(s8[8388608]{0:T(1024)(128)(4,1)} %bitcast.10), calls=%async_computation.13 | async-start | bytes 8388608
  28.0 12.5 %copy-start.4 = (s32[32,128]{1,0:T(8,128)S(1)}, s32[32,128]{1,0:T(8,128)}, u32[]{:S(2)}) copy-start(s32[32,128]{1,0:T(8,128)} %page_ref.1) | copy-start | bytes 49156
  28.0 12.5 %copy-start.5 = (s32[32]{0:T(128)S(1)}, s32[32]{0:T(128)}, u32[]{:S(2)}) copy-start(s32[32]{0:T(128)} %perm_ref.1) | copy-start | bytes 388
  28.1 12.5 %copy-start.6 = (s32[32]{0:T(128)S(1)}, s32[32]{0:T(128)}, u32[]{:S(2)}) copy-start(s32[32]{0:T(128)} %len_ref.1) | copy-start | bytes 388
  28.1 12.5 %copy-start.8 = (f32[1,128]{1,0:T(1,128)S(1)}, f32[1,128]{1,0:T(1,128)}, u32[]{:S(2)}) copy-start(f32[1,128]{1,0:T(1,128)} %constant.8.inverse_ref) | copy-start | bytes 1540
  40.6 25.6 %copy-start.3 = (bf16[320,640]{1,0:T(8,128)(2,1)S(1)}, bf16[320,640]{1,0:T(8,128)(2,1)}, u32[]{:S(2)}) copy-start(bf16[320,640]{1,0:T(8,128)(2,1)} %w_ref.2) | copy-start | bytes 1228804
  45.9 32.1 %copy-start.7 = (f32[40]{0:T(128)S(1)}, f32[40]{0:T(128)}, u32[]{:S(2)}) copy-start(f32[40]{0:T(128)} %param.25) | copy-start | bytes 484
  45.9 43.7 %copy-start.1 = (bf16[640,864]{0,1:T(8,128)(2,1)S(1)}, bf16[640,864]{0,1:T(8,128)(2,1)}, u32[]{:S(2)}) copy-start(bf16[640,864]{0,1:T(8,128)(2,1)} %param.27) | copy-start | bytes 3317764
  57.5 32.1 %copy-start = (bf16[640,864]{0,1:T(8,128)(2,1)S(1)}, bf16[640,864]{0,1:T(8,128)(2,1)}, u32[]{:S(2)}) copy-start(bf16[640,864]{0,1:T(8,128)(2,1)} %param.26) | copy-start | bytes 3317764
  90.4 1.6 %collective-permute-start = (bf16[4,16,1792]{2,1,0:T(8,128)(2,1)S(1)}, bf16[4,16,1792]{2,1,0:T(8,128)(2,1)S(1)}, u32[]{:S(2)}, u32[]{:S(2)}) collective-permute-start(bf16[4,16,1792]{2,1,0:T(8,128)(2,1)S(1)} %give_kernel.1), channel_id=1, source_target_pairs={{0,16},{16,0},{32,48},{48,32},{64,80},{80,64},{96,112},{112,96},{1... | collective-permute-start | bytes 688136 | tf_op jit(solution)/shard_map/ppermute | solution.py:426
  91.3 19.9 %copy-start.2 = (bf16[864,640]{1,0:T(8,128)(2,1)S(1)}, bf16[864,640]{1,0:T(8,128)(2,1)}, u32[]{:S(2)}) copy-start(bf16[864,640]{1,0:T(8,128)(2,1)} %w_ref.3) | copy-start | bytes 3317764
